TPU v7x, 512 devices: a whole 4x4x16 slice. The times are simulated.
512 devices in a mesh: tok: 32 (over y, x, core), voc: 16 (over z).
Axes of the slice: x: 4, y: 4, z: 16, core: 2. Of those that a mesh axis runs over, the one named last changes fastest.
Arguments:
- student_hidden: bfloat16 [512, 2560], P('tok', 'voc'), may hold values from -72 to 72
- teacher_rows: bfloat16 [512, 4096], P('tok', 'voc'), may hold values from -72 to 72
- student_head: bfloat16 [2560, 131072], P(None, ('tok', 'voc')), may hold values from -0.375 to 0.375
- teacher_head: bfloat16 [4096, 131072], P(None, ('tok', 'voc')), may hold values from -0.25 to 0.25
- lengths: int32 [32], replicated, may hold values from 1 to 16, 320 in all
- route: int32 [512], replicated, may hold values from 0 to 511, each once
- sampled_ids: int32 [512], replicated, may hold values from 0 to 131071
- mix_flags: int32 [512], replicated, may hold values 0 or 1
Outputs:
- divergence: float32 [512], P('tok')
- head_grad: bfloat16 [2560, 131072], P(None, ('tok', 'voc'))
Inputs may be any that keep to these rules, and one draw needn't show every extreme that they name: The lengths sum to 320; the largest is exactly 16. `route`: each trainer position appears once.
All inputs are finite; a program needn't handle non-finite values.
Results may differ from a plain program's by a relative error of at most 0.0052.
Values may be sent and summed in bfloat16 or wider, within the bound.
No kernel may reach another device: no remote copies, remote signals or barrier semaphores. Data moves between devices by JAX's collectives and lax.ppermute only.
A program may use at most 64 MiB of HBM per device.

v0:
```python
import jax
import jax.numpy as jnp
from jax import lax
from jax.sharding import PartitionSpec as P


def on_device(
    student_hidden, teacher_rows, student_head, teacher_head, lengths, route, sampled_ids, mix_flags
):
    tok_count = lax.axis_size("tok")
    voc_count = lax.axis_size("voc")
    group = lax.axis_index("tok")
    grp_rows = student_hidden.shape[0]
    vocab_dev = student_head.shape[1]
    first_col = (group * voc_count + lax.axis_index("voc")) * vocab_dev
    local_s, local_t = (student_hidden, teacher_rows)
    trainer_of = jnp.arange(grp_rows * tok_count, dtype=jnp.int32)
    live_rows = (trainer_of % grp_rows < lengths[trainer_of // grp_rows]).astype(jnp.float32)
    full_s, full_t = (
        lax.all_gather(local_s, "voc", axis=1, tiled=True),
        lax.all_gather(local_t, "voc", axis=1, tiled=True),
    )
    rows_s = lax.all_gather(full_s, "tok", axis=0, tiled=True)
    gathered = jnp.dot(
        lax.all_gather(full_t, "tok", axis=0, tiled=True),
        teacher_head,
        preferred_element_type=jnp.float32,
    )
    inverse = jnp.zeros_like(route).at[route].set(jnp.arange(route.shape[0], dtype=jnp.int32))
    teacher_logits = gathered[inverse]
    student_logits = jnp.dot(rows_s, student_head, preferred_element_type=jnp.float32)
    row_ids = sampled_ids[trainer_of]
    row_flags = mix_flags[trainer_of]
    onehot = row_ids[:, None] - first_col == jnp.arange(vocab_dev, dtype=jnp.int32)[None, :]
    pick_s = jnp.sum(jnp.where(onehot, student_logits, 0.0), axis=1)
    pick_u = jnp.sum(jnp.where(onehot, teacher_logits, 0.0), axis=1)
    s_max, u_max = lax.pmax(
        (jnp.max(student_logits, axis=1), jnp.max(teacher_logits, axis=1)), ("tok", "voc")
    )
    s_sum = jnp.sum(jnp.exp(student_logits - s_max[:, None]), axis=1)
    u_sum = jnp.sum(jnp.exp(teacher_logits - u_max[:, None]), axis=1)
    s_tot, u_tot, pick_s, pick_u = lax.psum((s_sum, u_sum, pick_s, pick_u), ("tok", "voc"))
    lse_s = s_max + jnp.log(s_tot)
    lse_u = u_max + jnp.log(u_tot)
    log_student = student_logits - lse_s[:, None]
    log_teacher = teacher_logits - lse_u[:, None]
    probs = jnp.exp(log_student)
    gap = log_student - log_teacher
    kl_all = lax.psum(jnp.sum(probs * gap, axis=1), ("tok", "voc"))
    mixed = 1.0 / (0.2 * jnp.exp(pick_u - lse_u - (pick_s - lse_s)) + 0.8)
    weight = jnp.where(row_flags == 1, mixed, jnp.ones_like(mixed))
    dlogits = ((live_rows * weight)[:, None] * probs * (gap - kl_all[:, None])).astype(jnp.bfloat16)
    head_grad = lax.dot_general(
        rows_s, dlogits, (((0,), (0,)), ((), ())), preferred_element_type=jnp.float32
    )
    kl_rows = live_rows * kl_all
    divergence = lax.dynamic_slice_in_dim(kl_rows, group * grp_rows, grp_rows)
    return (divergence, head_grad.astype(jnp.bfloat16))


def solution(mesh):
    in_specs = (
        P("tok", "voc"),
        P("tok", "voc"),
        P(None, ("tok", "voc")),
        P(None, ("tok", "voc")),
        P(),
        P(),
        P(),
        P(),
    )
    out_specs = (P("tok"), P(None, ("tok", "voc")))
    return jax.shard_map(
        on_device, mesh=mesh, in_specs=in_specs, out_specs=out_specs, check_vma=False
    )
```

profile of v0, /device:TPU:1, one launch (start us, length us, event | category | flops | bytes accessed | tf_op | source)
XLA Modules:
  0.0 505.5 jit_solution(3653330909238869689)
XLA Ops:
  7.2 0.0 copy-start
  7.2 0.0 copy-start.1
  7.2 0.0 all-gather.4.cloned.1.call-start
  7.3 30.2 %all-gather = bf16[16,160,16]{1,2,0:T(8,128)(2,1)S(1)} all-gather(bf16[1,160,16]{1,2,0:T(8,128)(2,1)} %bitcast.47), channel_id=1, replica_groups=mesh['tok'=32,'voc'=16] {'voc'}, dimensions={0}, use_global_device_ids=true | all-gather | bytes 87040 | tf_op jit(solution)/shard_map/all_gather | solution.py:20
  37.5 0.8 reshape.200
  38.3 0.0 all-gather.4.cloned.1.call-update
  38.4 0.0 all-gather.6.cloned.1.call-start
  38.4 22.4 %all_gather.14 = bf16[16,4096]{1,0:T(8,128)(2,1)} all-gather(bf16[16,256]{1,0:T(8,128)(2,1)} %param.9), channel_id=1, replica_groups=mesh['tok'=32,'voc'=16] {'voc'}, dimensions={1}, use_global_device_ids=true | all-gather | bytes 139264 | tf_op jit(solution)/shard_map/all_gather | solution.py:21
  60.8 0.0 all-gather.6.cloned.1.call-update
  60.8 3.6 gather_fusion.2
  64.4 3.5 gather_fusion.1
  68.0 2.4 scatter_custom_fusion
  71.3 0.7 fusion.14
  72.0 4.3 compare_select_fusion.1
  76.4 0.7 fusion.13
  77.1 24.5 %all-gather.4.cloned.1.call-done = bf16[512,2560]{1,0:T(8,128)(2,1)} async-done(((bf16[16,2560]{1,0:T(8,128)(2,1)}), bf16[512,2560]{1,0:T(8,128)(2,1)}) %all-gather.4.cloned.1.call-update) | async-done | bytes 2621456 | tf_op jit(solution)/shard_map/all_gather | solution.py:23
  101.6 3.8 fusion.15
  105.4 60.2 %all-gather.6.cloned.1.call-done = bf16[512,4096]{1,0:T(8,128)(2,1)} async-done(((bf16[16,4096]{1,0:T(8,128)(2,1)}), bf16[512,4096]{1,0:T(8,128)(2,1)}) %all-gather.6.cloned.1.call-update) | async-done | bytes 4194320 | tf_op jit(solution)/shard_map/all_gather | solution.py:25
  165.6 3.4 fusion.16
  169.1 1.6 gather_fusion
  170.7 1.0 copy.18
  171.7 0.1 reduce_max.19
  171.8 103.7 %all-reduce.2 = (f32[512]{0:T(512)S(1)}, f32[512]{0:T(512)S(1)}) all-reduce(f32[512]{0:T(512)S(1)} %reduce_max.19, f32[512]{0:T(512)S(1)} %get-tuple-element.52), channel_id=1, replica_groups=mesh['tok'=32,'voc'=16] {'tok','voc'}, use_global_device_ids=true, to_apply=%region_6.7 | all-reduce | flops 1024 | bytes 8192 | tf_op jit(solution)/shard_map/pmax | solution.py:37
  275.5 0.2 exponential_reduce_fusion
  275.7 1.2 exponential_reduce_fusion.1
  276.9 100.3 %all-reduce.1 = (f32[512]{0:T(512)S(1)}, f32[512]{0:T(512)S(1)}) all-reduce(f32[512]{0:T(512)S(1)} %exponential_reduce_fusion, f32[512]{0:T(512)S(1)} %exponential_reduce_fusion.1), channel_id=1, replica_groups=mesh['tok'=32,'voc'=16] {'tok','voc'}, use_global_device_ids=true, to_apply=%region_8.9 | all-reduce | flops 1024 | bytes 8192 | tf_op jit(solution)/shard_map/psum | solution.py:42
  377.2 1.3 select_reduce_fusion.1
  378.5 99.5 %all-reduce = (f32[512]{0:T(512)S(1)}, f32[512]{0:T(512)S(1)}, f32[512]{0:T(512)S(1)}) all-reduce(f32[512]{0:T(512)S(1)} %get-tuple-element.9, f32[512]{0:T(512)S(1)} %get-tuple-element.10, f32[512]{0:T(512)S(1)} %get-tuple-element.8), channel_id=1, replica_groups=mesh['tok'=32,'voc'=16] {'tok','voc'}, use_global_device_ids=true, to_apply=%region_10.11 | all-reduce | flops 1536 | bytes 12288 | tf_op jit(solution)/shard_map/psum | solution.py:49
  478.0 15.7 %fusion.5 = (f32[512]{0:T(512)S(1)}, pred[512]{0:T(512)(128)(4,1)S(1)}) fusion(f32[512]{0:T(512)S(1)} %get-tuple-element.12, f32[512]{0:T(512)S(1)} %get-tuple-element.55, f32[512]{0:T(512)S(1)} %get-tuple-element.13, f32[512]{0:T(512)S(1)} %get-tuple-element.54, s32[512]{0:T(512)S(1)} %gather_fusion.1, pred[512]{0:T(512)(128)(4,1)S(1)} %compare_reduce_fusion, ...), kind=kLoop, calls=%fused_computation.60 | loop fusion | flops 20992 | bytes 27748 | tf_op jit(solution)/shard_map/mul | solution.py:52
  493.7 2.9 fusion
  496.7 1.4 copy.20
  498.1 0.6 dynamic_slice.3
  (43 shorter events, 1.0 us)
Async XLA Ops:
  7.2 158.5 %copy-start = (bf16[4096,256]{1,0:T(8,128)(2,1)S(1)}, bf16[4096,256]{1,0:T(8,128)(2,1)}, u32[]{:S(2)}) copy-start(bf16[4096,256]{1,0:T(8,128)(2,1)} %param.11) | copy-start | bytes 6291460
  7.2 57.3 %copy-start.1 = (s32[512]{0:T(512)S(1)}, s32[512]{0:T(512)}, u32[]{:S(2)}) copy-start(s32[512]{0:T(512)} %param.15) | copy-start | bytes 6148
  7.2 60.8 %copy-start.4 = (s32[512]{0:T(512)S(1)}, s32[512]{0:T(512)}, u32[]{:S(2)}) copy-start(s32[512]{0:T(512)} %param.13) | copy-start | bytes 6148
  7.2 94.4 %all-gather.4.cloned.1.call-start = ((), (), s32[]{:S(2)}) async-start(), calls=%async_computation | async-start | bytes 2703360 | tf_op jit(solution)/shard_map/all_gather | solution.py:23
  7.2 64.0 %copy-start.3 = (s32[32]{0:T(128)S(1)}, s32[32]{0:T(128)}, u32[]{:S(2)}) copy-start(s32[32]{0:T(128)} %param.12) | copy-start | bytes 388
  38.4 127.3 %all-gather.6.cloned.1.call-start = ((), (), s32[]{:S(2)}) async-start(), calls=%async_computation.1 | async-start | bytes 4325376 | tf_op jit(solution)/shard_map/all_gather | solution.py:25
  170.7 206.5 %copy-start.2 = (f32[512,256]{0,1:T(8,128)S(1)}, f32[512,256]{0,1:T(8,128)}, u32[]{:S(2)}) copy-start(f32[512,256]{0,1:T(8,128)} %get-tuple-element.53) | copy-start | bytes 1572868
Sparse Core Ops, SparseCore 0:
  38.5 63.0 all-gather.3
  104.7 60.8 all-gather.5
where the time goes:
time: 506 us
  blocking collectives  356 us (70%)
  waiting for transfers between devices  84.7 us (17%)
  other arithmetic  23.8 us (5%)
  local copies, waits for them, and re-layouts  16.5 us (3%)
  between operations  14.2 us (3%)
  matrix products  10.2 us (2%)
    pmax x1, blocking collectives, on_device(): lax.pmax((jnp.max(student_logits, axis=1), jnp.max(teacher_logits, axis=1...  104 us
    psum x1, blocking collectives, on_device(): lax.psum((s_sum, u_sum, pick_s, pick_u), ('tok', 'voc'))  100 us
    psum x1, blocking collectives, on_device(): kl_all = lax.psum(jnp.sum(probs * gap, axis=1), ('tok', 'voc'))  99.5 us
    all_gather x1, waiting for transfers between devices, on_device(): lax.all_gather(full_t, 'tok', axis=0, tiled=True)  60.2 us
    all_gather x1, blocking collectives, on_device(): lax.all_gather(local_s, 'voc', axis=1, tiled=True)  30.2 us
    all_gather x1, waiting for transfers between devices, on_device(): rows_s = lax.all_gather(full_s, 'tok', axis=0, tiled=True)  24.5 us
    all_gather x1, blocking collectives, on_device(): lax.all_gather(local_t, 'voc', axis=1, tiled=True)  22.4 us
    mul x1, other arithmetic, on_device(): live_rows * weight  15.7 us
  transfers between devices with their start and end apart: 2, of which 2 were waited for; matrix products, arithmetic and copies ran while one was open for 4% of the time, Pallas kernels for 0%

commit v1 on v0

v1 whole, which is shorter than its diff:
```python
import jax
import jax.numpy as jnp
from jax import lax
from jax.experimental import pallas as pl
from jax.experimental.pallas import tpu as pltpu
from jax.sharding import Mesh, PartitionSpec as P

F32 = jnp.float32
BF16 = jnp.bfloat16
VMEM = pl.BlockSpec(memory_space=pltpu.VMEM)
SMEM = pl.BlockSpec(memory_space=pltpu.SMEM)
LIMIT = pltpu.CompilerParams(vmem_limit_bytes=56 * 1024 * 1024)


def spread_kernel(gathered, out):
    nz = gathered.shape[0]
    teacher = [gathered[z, :, :256] for z in range(nz)]
    student = [gathered[z, :, 256:] for z in range(nz)]
    whole = jnp.concatenate(teacher + student, axis=1)
    for i in range(out.shape[0]):
        out[i] = whole


def half_kernel(rows, head_s, head_t, s_out, u_out):
    dt = head_t.shape[0]
    s_out[...] = jnp.dot(rows[:, dt:], head_s[...], preferred_element_type=F32)
    u_out[...] = jnp.dot(rows[:, :dt], head_t[...], preferred_element_type=F32)


def store_stats(out, values):
    for k, value in enumerate(values):
        tiles = value.shape[1] // 128
        for j in range(tiles):
            out[k * tiles + j : k * tiles + j + 1, :] = value[:, 128 * j : 128 * j + 128]


def stats_kernel(
    where, rows, head_s, head_t, s_own, u_own, route, ids, s_t_out, u_t_out, stats_out, s_nat, u_nat
):
    core, first_col = where[0], where[1]
    dt = head_t.shape[0]
    tokens = s_nat.shape[0]
    halves = (
        (core, s_own[...], u_own[...]),
        (
            1 - core,
            jnp.dot(rows[:, dt:], head_s[...], preferred_element_type=F32),
            jnp.dot(rows[:, :dt], head_t[...], preferred_element_type=F32),
        ),
    )
    for half, s_half, u_half in halves:
        for j in range(tokens // 32):
            at = pl.ds(pl.multiple_of((2 * j + half) * 16, 16), 16)
            s_nat[at, :] = s_half[16 * j : 16 * j + 16]
            u_nat[at, :] = u_half[16 * j : 16 * j + 16]
    s_t = s_nat[...].T
    u_roll = u_nat[...].T
    order = lax.broadcasted_iota(jnp.int32, (tokens, tokens), 0)
    pick = jnp.where(order == route[...], 1.0, 0.0).astype(BF16)
    high = u_roll.astype(BF16)
    rest = u_roll - high.astype(F32)
    middle = rest.astype(BF16)
    low = (rest - middle.astype(F32)).astype(BF16)
    u_t = jnp.zeros_like(u_roll)
    for part in (low, middle, high):
        u_t = u_t + lax.dot_general(
            part, pick, (((1,), (1,)), ((), ())), preferred_element_type=F32
        )
    s_t_out[...] = s_t
    u_t_out[...] = u_t
    m_s = jnp.max(s_t, axis=0, keepdims=True)
    m_u = jnp.max(u_t, axis=0, keepdims=True)
    s_rel = s_t - m_s
    u_rel = u_t - m_u
    e_s = jnp.exp(s_rel)
    sum_s = jnp.sum(e_s, axis=0, keepdims=True)
    sum_u = jnp.sum(jnp.exp(u_rel), axis=0, keepdims=True)
    mean = jnp.sum(e_s * (s_rel - u_rel), axis=0, keepdims=True) / sum_s
    log_s = jnp.log(sum_s)
    log_u = jnp.log(sum_u)
    column = lax.broadcasted_iota(jnp.int32, s_t.shape, 0)
    hit = column == ids[...] - first_col
    apart = jnp.sum(jnp.where(hit, u_t - s_t, 0.0), axis=0, keepdims=True)
    store_stats(stats_out, (m_s + log_s, m_u + log_u, mean - log_s + log_u, apart))


def merge(parts):
    lse_s, lse_u = parts[:, 0:4], parts[:, 4:8]
    kl, apart = parts[:, 8:12], parts[:, 12:16]
    m_s = jnp.max(lse_s, axis=0)
    m_u = jnp.max(lse_u, axis=0)
    all_s = m_s + jnp.log(jnp.sum(jnp.exp(lse_s - m_s), axis=0))
    all_u = m_u + jnp.log(jnp.sum(jnp.exp(lse_u - m_u), axis=0))
    share = jnp.exp(lse_s - all_s)
    whole = jnp.sum(share * (kl + (lse_s - all_s) - (lse_u - all_u)), axis=0)
    return all_s, all_u, whole, jnp.sum(apart, axis=0)


def merge_kernel(parts, out):
    merged = jnp.concatenate(merge(parts[...]), axis=0)
    for i in range(out.shape[0]):
        out[i] = merged


def grad_kernel(
    where, lengths, parts, s_t, u_t, flags, own, other, kl_out, grad_out, dl_nat, dl_half
):
    core = where[0]
    tokens = dl_nat.shape[0]
    dt = own.shape[1] - grad_out.shape[0]

    def lanes(rows):
        return jnp.concatenate([rows[j : j + 1] for j in range(4)], axis=1)

    lse_s, lse_u, kl, apart = [lanes(v) for v in merge(parts[...])]
    slot = lax.broadcasted_iota(jnp.int32, (1, tokens), 1)
    length = jnp.zeros((1, tokens), jnp.int32)
    for w in range(lengths.shape[0]):
        length = jnp.where(slot // 16 == w, lengths[w], length)
    live = (slot % 16 < length).astype(F32)
    mixed = 1.0 / (0.2 * jnp.exp(apart - lse_u + lse_s) + 0.8)
    weight = jnp.where(flags[...] == 1, mixed, jnp.ones_like(mixed))
    kl_out[...] = live * kl
    log_s = s_t[...] - lse_s
    gap = log_s - (u_t[...] - lse_u)
    d_t = (live * weight) * jnp.exp(log_s) * (gap - kl)
    dl_nat[...] = d_t.T
    for n, half in enumerate((core, 1 - core)):
        for j in range(tokens // 32):
            at = pl.ds(pl.multiple_of((2 * j + half) * 16, 16), 16)
            dl_half[n, 16 * j : 16 * j + 16, :] = dl_nat[at, :].astype(BF16)
    step = 512
    for f in range(0, grad_out.shape[0], step):
        total = jnp.zeros((grad_out.shape[1], step), F32)
        for n, rows in enumerate((own, other)):
            total = total + lax.dot_general(
                dl_half[n], rows[:, dt + f : dt + f + step], (((0,), (0,)), ((), ())),
                preferred_element_type=F32,
            )
        grad_out[f : f + step, :] = total.T.astype(BF16)


def on_device(
    student_hidden, teacher_rows, student_head, teacher_head, lengths, route, sampled_ids, mix_flags
):
    ny, nx, nz = lax.axis_size("y"), lax.axis_size("x"), lax.axis_size("z")
    core = lax.axis_index("c")
    group = (lax.axis_index("y") * nx + lax.axis_index("x")) * 2 + core
    grp_rows = student_hidden.shape[0]
    ds, vocab_dev = student_head.shape
    dt = teacher_head.shape[0]
    tokens = route.shape[0]
    half = tokens // 2
    first_col = (group * nz + lax.axis_index("z")) * vocab_dev
    where = jnp.stack([core, first_col]).astype(jnp.int32)

    local = jnp.concatenate([teacher_rows, student_hidden], axis=1)
    gathered = lax.all_to_all(jnp.broadcast_to(local, (nz,) + local.shape), "z", 0, 0)
    copies = pl.pallas_call(
        spread_kernel,
        out_shape=jax.ShapeDtypeStruct((ny * nx, grp_rows, dt + ds), BF16),
        in_specs=[VMEM], out_specs=VMEM, compiler_params=LIMIT,
    )(gathered)
    own = lax.all_to_all(copies, ("y", "x"), 0, 0).reshape(half, dt + ds)
    other = lax.ppermute(own, "c", [(0, 1), (1, 0)])
    logits = jax.ShapeDtypeStruct((half, vocab_dev), F32)
    s_own, u_own = pl.pallas_call(
        half_kernel, out_shape=(logits, logits),
        in_specs=[VMEM] * 3, out_specs=(VMEM, VMEM), compiler_params=LIMIT,
    )(own, student_head, teacher_head)
    whole = jax.ShapeDtypeStruct((vocab_dev, tokens), F32)
    s_t, u_t, stats = pl.pallas_call(
        stats_kernel,
        out_shape=(whole, whole, jax.ShapeDtypeStruct((4 * tokens // 128, 128), F32)),
        in_specs=[SMEM] + [VMEM] * 7, out_specs=(VMEM,) * 3,
        scratch_shapes=[pltpu.VMEM((tokens, vocab_dev), F32)] * 2, compiler_params=LIMIT,
    )(where, other, student_head, teacher_head, s_own, u_own, route[None], sampled_ids[None])
    near = lax.all_to_all(jnp.broadcast_to(stats, (2 * ny * nx,) + stats.shape), ("y", "x", "c"), 0, 0)
    merged = pl.pallas_call(
        merge_kernel,
        out_shape=jax.ShapeDtypeStruct((nz,) + stats.shape, F32),
        in_specs=[VMEM], out_specs=VMEM,
    )(near)
    far = lax.all_to_all(merged, "z", 0, 0)
    kl_rows, head_grad = pl.pallas_call(
        grad_kernel,
        out_shape=(
            jax.ShapeDtypeStruct((1, tokens), F32),
            jax.ShapeDtypeStruct((ds, vocab_dev), BF16),
        ),
        in_specs=[SMEM] * 2 + [VMEM] * 6, out_specs=(VMEM,) * 2,
        scratch_shapes=[
            pltpu.VMEM((tokens, vocab_dev), F32), pltpu.VMEM((2, half, vocab_dev), BF16)
        ],
        compiler_params=LIMIT,
    )(where, lengths, far, s_t, u_t, mix_flags[None], own, other)
    divergence = lax.dynamic_slice_in_dim(kl_rows[0], group * grp_rows, grp_rows)
    return divergence, head_grad


def solution(mesh):
    fine = Mesh(mesh.devices.reshape(4, 4, 2, 16), ("y", "x", "c", "z"))
    tok = ("y", "x", "c")
    every = tok + ("z",)
    in_specs = (P(tok, "z"), P(tok, "z"), P(None, every), P(None, every), P(), P(), P(), P())
    out_specs = (P(tok), P(None, every))
    return jax.shard_map(
        on_device, mesh=fine, in_specs=in_specs, out_specs=out_specs, check_vma=False
    )
```

time: 506 us -> 145 us (0.29)
  blocking collectives: 356 us -> 85.8 us
  waiting for transfers between devices: 84.7 us -> 12.4 us
  other arithmetic: 23.8 us -> 1.39 us
  Pallas kernels: 0 us -> 21.6 us
  starting transfers between devices: 0.08 us -> 18.6 us
  local copies, waits for them, and re-layouts: 16.5 us -> 2.62 us
  between operations: 14.2 us -> 0.68 us
  matrix products: 10.2 us -> 0 us
    psum x2 -> x0, blocking collectives: 200 us -> none  [the longest x1 100 us: on_device(): lax.psum((s_sum, u_sum, pick_s, pick_u), ('tok', 'voc'))]
    pmax x1 -> x0, blocking collectives: 104 us -> none  [on_device(): lax.pmax((jnp.max(student_logits, axis=1), jnp.max(teacher_logits, axis=1...]
    all_to_all x0 -> x3, blocking collectives: none -> 85.8 us  [the longest x1 43.8 us: on_device(): own = lax.all_to_all(copies, ('y', 'x'), 0, 0).reshape(half, dt + ds)]
    all_gather x2 -> x0, waiting for transfers between devices: 84.7 us -> none  [the longest x1 60.2 us: on_device(): lax.all_gather(full_t, 'tok', axis=0, tiled=True)]
    all_gather x2 -> x0, blocking collectives: 52.6 us -> none  [the longest x1 30.2 us: on_device(): lax.all_gather(local_s, 'voc', axis=1, tiled=True)]
    pallas_call x0 -> x5, Pallas kernels: none -> 21.6 us  [the longest x1 6.45 us: on_device(): pl.pallas_call(stats_kernel, out_shape=(whole, whole, jax.ShapeDtypeStruc...]
    mul x2 -> x0, other arithmetic: 15.7 us -> none  [the longest x1 15.7 us: on_device(): live_rows * weight]
    all_to_all x0 -> x1, waiting for transfers between devices: none -> 12.1 us  [on_device(): far = lax.all_to_all(merged, 'z', 0, 0)]
  transfers between devices with their start and end apart: 2 -> 2, of which waited for: 2 -> 2; matrix products, arithmetic and copies ran while one was open for 4% -> 0% of each run, Pallas kernels for 0% -> 3%
where the time goes in v1:
time: 145 us; the launch traced here: 143 us
  blocking collectives  85.8 us (59%)
  Pallas kernels  21.6 us (15%)
  starting transfers between devices  18.6 us (13%)
  waiting for transfers between devices  12.4 us (9%)
  local copies, waits for them, and re-layouts  2.62 us (2%)
    all_to_all x1, blocking collectives, on_device(): own = lax.all_to_all(copies, ('y', 'x'), 0, 0).reshape(half, dt + ds)  43.8 us
    all_to_all x1, blocking collectives, on_device(): lax.all_to_all(jnp.broadcast_to(local, (nz,) + local.shape), 'z', 0, 0)  29.4 us
    all_to_all x1, blocking collectives, on_device(): lax.all_to_all(jnp.broadcast_to(stats, (2 * ny * nx,) + stats.shape), ('y...  12.7 us
    all_to_all x1, waiting for transfers between devices, on_device(): far = lax.all_to_all(merged, 'z', 0, 0)  12.1 us
    all_to_all x1, starting transfers between devices, on_device(): far = lax.all_to_all(merged, 'z', 0, 0)  10 us
    ppermute x1, starting transfers between devices, on_device(): other = lax.ppermute(own, 'c', [(0, 1), (1, 0)])  8.54 us
    pallas_call x1, Pallas kernels, on_device(): pl.pallas_call(stats_kernel, out_shape=(whole, whole, jax.ShapeDtypeStruc...  6.45 us
    pallas_call x1, Pallas kernels, on_device(): pl.pallas_call(grad_kernel, out_shape=(jax.ShapeDtypeStruct((1, tokens),...  5.72 us
  transfers between devices with their start and end apart: 2, of which 2 were waited for; matrix products, arithmetic and copies ran while one was open for 0% of the time, Pallas kernels for 3%

profile of v1, /device:TPU:1, one launch (start us, length us, event | category | flops | bytes accessed | tf_op | source)
XLA Modules:
  0.0 143.2 jit_solution(16720293305906863868)
XLA Ops:
  0.6 0.7 pad_maximum_fusion
  1.4 29.4 %all_to_all.20.gathered = bf16[16,16,416]{2,1,0:T(8,128)(2,1)} all-to-all(bf16[16,16,416]{2,1,0:T(8,128)(2,1)S(1)} %broadcast_in_dim.15), channel_id=1, replica_groups=mesh['y'=4,'x'=4,'c'=2,'z'=16] {'z'}, dimensions={0} | all-to-all | bytes 425984 | tf_op jit(solution)/shard_map/all_to_all | solution.py:158
  30.8 2.9 %shard_map.95 = bf16[16,16,6656]{2,1,0:T(8,128)(2,1)} custom-call(bf16[16,16,416]{2,1,0:T(8,128)(2,1)} %all_to_all.20.gathered), custom_call_target="tpu_custom_call" | custom-call | tf_op jit(solution)/shard_map/pallas_call | solution.py:159
  33.7 43.8 %all_to_all.21 = bf16[16,16,6656]{2,1,0:T(8,128)(2,1)S(1)} all-to-all(bf16[16,16,6656]{2,1,0:T(8,128)(2,1)} %shard_map.95), channel_id=1, replica_groups=mesh['y'=4,'x'=4,'c'=2,'z'=16] {'y','x'}, dimensions={0} | all-to-all | bytes 6815744 | tf_op jit(solution)/shard_map/all_to_all | solution.py:164
  77.5 0.0 copy-start
  77.5 8.5 %collective-permute-start = (bf16[256,6656]{1,0:T(8,128)(2,1)S(1)}, bf16[256,6656]{1,0:T(8,128)(2,1)}, u32[]{:S(2)}, u32[]{:S(2)}) collective-permute-start(bf16[256,6656]{1,0:T(8,128)(2,1)S(1)} %bitcast.8), channel_id=1, source_target_pairs={{0,16},{16,0},{1,17},{17,1},{2,18},{18,2},{3,19},{19,3},{4,20},{20... | collective-permute-start | bytes 10223624 | tf_op jit(solution)/shard_map/ppermute | solution.py:165
  86.0 0.7 pad_add_fusion.where
  86.7 0.0 copy-done
  86.7 4.8 %shard_map.96 = (f32[256,256]{1,0:T(8,128)}, f32[256,256]{1,0:T(8,128)}) custom-call(bf16[256,6656]{1,0:T(8,128)(2,1)} %bitcast.9, bf16[2560,256]{1,0:T(8,128)(2,1)} %head_s.3, bf16[4096,256]{1,0:T(8,128)(2,1)} %head_t.3), custom_call_target="tpu_custom_call" | custom-call | tf_op jit(solution)/shard_map/pallas_call | solution.py:167
  91.5 0.3 collective-permute-done.rows.other
  91.8 6.5 %shard_map.97 = (f32[256,512]{1,0:T(8,128)}, f32[256,512]{1,0:T(8,128)}, f32[16,128]{1,0:T(8,128)}) custom-call(s32[2]{0:T(128)} %pad_add_fusion.where, bf16[256,6656]{1,0:T(8,128)(2,1)} %collective-permute-done.rows.other, bf16[2560,256]{1,0:T(8,128)(2,1)} %head_s.3, bf16[4096,256]{1,0:T(8,128)(2,1)} %head_t.3, f32[256,256]{1,0:T(8,128)} %get-tuple-element.9.s_own, ...), custom_call_target="tpu_custom_call" | custom-call | tf_op jit(solution)/shard_map/pallas_call | solution.py:172
  98.2 0.7 broadcast_in_dim.18
  99.0 12.7 %all_to_all.22.parts = f32[32,16,128]{2,1,0:T(8,128)} all-to-all(f32[32,16,128]{2,1,0:T(8,128)S(1)} %broadcast_in_dim.18), channel_id=1, replica_groups=mesh['y'=4,'x'=4,'c'=2,'z'=16] {'y','x','c'}, dimensions={0} | all-to-all | bytes 524288 | tf_op jit(solution)/shard_map/all_to_all | solution.py:178
  111.6 1.7 %shard_map.98 = f32[16,16,128]{2,1,0:T(8,128)} custom-call(f32[32,16,128]{2,1,0:T(8,128)} %all_to_all.22.parts), custom_call_target="tpu_custom_call" | custom-call | tf_op jit(solution)/shard_map/pallas_call | solution.py:179
  113.4 10.0 %all-to-all-start.3 = ((f32[16,16,128]{2,1,0:T(8,128)}), f32[16,16,128]{2,1,0:T(8,128)S(1)}, u32[]{:S(2)}, u32[]{:S(2)}) async-start(f32[16,16,128]{2,1,0:T(8,128)} %shard_map.98), calls=%async_computation.3 | async-start | bytes 262144 | tf_op jit(solution)/shard_map/all_to_all | solution.py:184
  123.4 12.1 %all-to-all-done.3.parts = f32[16,16,128]{2,1,0:T(8,128)S(1)} async-done(((f32[16,16,128]{2,1,0:T(8,128)}), f32[16,16,128]{2,1,0:T(8,128)S(1)}, u32[]{:S(2)}, u32[]{:S(2)}) %all-to-all-start.3) | async-done | bytes 131104 | tf_op jit(solution)/shard_map/all_to_all | solution.py:184
  135.5 0.0 copy-start.1
  135.5 0.6 copy-done.1
  136.2 5.7 %shard_map.99 = (f32[1,512]{1,0:T(1,128)}, bf16[2560,256]{1,0:T(8,128)(2,1)}) custom-call(s32[2]{0:T(128)} %pad_add_fusion.where, s32[32]{0:T(128)} %lengths.1, f32[16,16,128]{2,1,0:T(8,128)} %copy-done.1, f32[256,512]{1,0:T(8,128)} %get-tuple-element.12.s_t, f32[256,512]{1,0:T(8,128)} %get-tuple-element.13.u_t, s32[1,512]{1,0:T(1,128)} %bitcast.13, ...), custom_call_target="tpu_custom_call" | custom-call | tf_op jit(solution)/shard_map/pallas_call | solution.py:185
  141.9 1.2 dynamic-slice_bitcast_fusion
  (1 shorter events, 0.0 us)
Async XLA Ops:
  77.5 9.2 %copy-start = (bf16[16,16,6656]{2,1,0:T(8,128)(2,1)}, bf16[16,16,6656]{2,1,0:T(8,128)(2,1)S(1)}, u32[]{:S(2)}) copy-start(bf16[16,16,6656]{2,1,0:T(8,128)(2,1)S(1)} %all_to_all.21) | copy-start | bytes 10223620
  77.5 14.3 %collective-permute-start = (bf16[256,6656]{1,0:T(8,128)(2,1)S(1)}, bf16[256,6656]{1,0:T(8,128)(2,1)}, u32[]{:S(2)}, u32[]{:S(2)}) collective-permute-start(bf16[256,6656]{1,0:T(8,128)(2,1)S(1)} %bitcast.8), channel_id=1, source_target_pairs={{0,16},{16,0},{1,17},{17,1},{2,18},{18,2},{3,19},{19,3},{4,20},{20... | collective-permute-start | bytes 10223624 | tf_op jit(solution)/shard_map/ppermute | solution.py:165
  113.4 22.2 %all-to-all-start.3 = ((f32[16,16,128]{2,1,0:T(8,128)}), f32[16,16,128]{2,1,0:T(8,128)S(1)}, u32[]{:S(2)}, u32[]{:S(2)}) async-start(f32[16,16,128]{2,1,0:T(8,128)} %shard_map.98), calls=%async_computation.3 | async-start | bytes 262144 | tf_op jit(solution)/shard_map/all_to_all | solution.py:184
  135.5 0.6 copy-start.1

commit v2 on v1

--- a/solution.py
+++ b/solution.py
@@ -9,7 +9,10 @@
 BF16 = jnp.bfloat16
 VMEM = pl.BlockSpec(memory_space=pltpu.VMEM)
 SMEM = pl.BlockSpec(memory_space=pltpu.SMEM)
-LIMIT = pltpu.CompilerParams(vmem_limit_bytes=56 * 1024 * 1024)
+
+
+def grant(mib):
+    return pltpu.CompilerParams(vmem_limit_bytes=mib * 1024 * 1024)
 
 
 def spread_kernel(gathered, out):
@@ -28,10 +31,10 @@
 
 
 def store_stats(out, values):
-    for k, value in enumerate(values):
-        tiles = value.shape[1] // 128
-        for j in range(tiles):
-            out[k * tiles + j : k * tiles + j + 1, :] = value[:, 128 * j : 128 * j + 128]
+    rows = [v[:, 128 * j : 128 * j + 128] for v in values for j in range(v.shape[1] // 128)]
+    block = jnp.concatenate(rows, axis=0)
+    for i in range(out.shape[0]):
+        out[i] = block
 
 
 def stats_kernel(
@@ -105,7 +108,7 @@
 def grad_kernel(
     where, lengths, parts, s_t, u_t, flags, own, other, kl_out, grad_out, dl_nat, dl_half
 ):
-    core = where[0]
+    core, group = where[0], where[2]
     tokens = dl_nat.shape[0]
     dt = own.shape[1] - grad_out.shape[0]
 
@@ -120,7 +123,11 @@
     live = (slot % 16 < length).astype(F32)
     mixed = 1.0 / (0.2 * jnp.exp(apart - lse_u + lse_s) + 0.8)
     weight = jnp.where(flags[...] == 1, mixed, jnp.ones_like(mixed))
-    kl_out[...] = live * kl
+    kl_rows = live * kl
+    mine = jnp.zeros((1, 16), F32)
+    for w in range(lengths.shape[0]):
+        mine = jnp.where(group == w, kl_rows[:, 16 * w : 16 * w + 16], mine)
+    kl_out[...] = mine
     log_s = s_t[...] - lse_s
     gap = log_s - (u_t[...] - lse_u)
     d_t = (live * weight) * jnp.exp(log_s) * (gap - kl)
@@ -152,50 +159,50 @@
     tokens = route.shape[0]
     half = tokens // 2
     first_col = (group * nz + lax.axis_index("z")) * vocab_dev
-    where = jnp.stack([core, first_col]).astype(jnp.int32)
+    where = jnp.stack([core, first_col, group]).astype(jnp.int32)
 
     local = jnp.concatenate([teacher_rows, student_hidden], axis=1)
     gathered = lax.all_to_all(jnp.broadcast_to(local, (nz,) + local.shape), "z", 0, 0)
     copies = pl.pallas_call(
         spread_kernel,
         out_shape=jax.ShapeDtypeStruct((ny * nx, grp_rows, dt + ds), BF16),
-        in_specs=[VMEM], out_specs=VMEM, compiler_params=LIMIT,
+        in_specs=[VMEM], out_specs=VMEM, compiler_params=grant(8),
     )(gathered)
     own = lax.all_to_all(copies, ("y", "x"), 0, 0).reshape(half, dt + ds)
     other = lax.ppermute(own, "c", [(0, 1), (1, 0)])
     logits = jax.ShapeDtypeStruct((half, vocab_dev), F32)
     s_own, u_own = pl.pallas_call(
         half_kernel, out_shape=(logits, logits),
-        in_specs=[VMEM] * 3, out_specs=(VMEM, VMEM), compiler_params=LIMIT,
+        in_specs=[VMEM] * 3, out_specs=(VMEM, VMEM), compiler_params=grant(8),
     )(own, student_head, teacher_head)
     whole = jax.ShapeDtypeStruct((vocab_dev, tokens), F32)
+    block = (4 * tokens // 128, 128)
     s_t, u_t, stats = pl.pallas_call(
         stats_kernel,
-        out_shape=(whole, whole, jax.ShapeDtypeStruct((4 * tokens // 128, 128), F32)),
+        out_shape=(whole, whole, jax.ShapeDtypeStruct((2 * ny * nx,) + block, F32)),
         in_specs=[SMEM] + [VMEM] * 7, out_specs=(VMEM,) * 3,
-        scratch_shapes=[pltpu.VMEM((tokens, vocab_dev), F32)] * 2, compiler_params=LIMIT,
+        scratch_shapes=[pltpu.VMEM((tokens, vocab_dev), F32)] * 2, compiler_params=grant(8),
     )(where, other, student_head, teacher_head, s_own, u_own, route[None], sampled_ids[None])
-    near = lax.all_to_all(jnp.broadcast_to(stats, (2 * ny * nx,) + stats.shape), ("y", "x", "c"), 0, 0)
+    near = lax.all_to_all(stats, ("y", "x", "c"), 0, 0)
     merged = pl.pallas_call(
         merge_kernel,
-        out_shape=jax.ShapeDtypeStruct((nz,) + stats.shape, F32),
-        in_specs=[VMEM], out_specs=VMEM,
+        out_shape=jax.ShapeDtypeStruct((nz,) + block, F32),
+        in_specs=[VMEM], out_specs=VMEM, compiler_params=grant(4),
     )(near)
     far = lax.all_to_all(merged, "z", 0, 0)
     kl_rows, head_grad = pl.pallas_call(
         grad_kernel,
         out_shape=(
-            jax.ShapeDtypeStruct((1, tokens), F32),
+            jax.ShapeDtypeStruct((1, grp_rows), F32),
             jax.ShapeDtypeStruct((ds, vocab_dev), BF16),
         ),
         in_specs=[SMEM] * 2 + [VMEM] * 6, out_specs=(VMEM,) * 2,
         scratch_shapes=[
             pltpu.VMEM((tokens, vocab_dev), F32), pltpu.VMEM((2, half, vocab_dev), BF16)
         ],
-        compiler_params=LIMIT,
+        compiler_params=grant(8),
     )(where, lengths, far, s_t, u_t, mix_flags[None], own, other)
-    divergence = lax.dynamic_slice_in_dim(kl_rows[0], group * grp_rows, grp_rows)
-    return divergence, head_grad
+    return kl_rows[0], head_grad
 
 
 def solution(mesh):

time: 145 us -> 135 us (0.931)
  blocking collectives: 85.8 us -> 107 us
  waiting for transfers between devices: 12.4 us -> 1.72 us
  starting transfers between devices: 18.6 us -> 8.54 us
  Pallas kernels: 21.6 us -> 11.8 us
    all_to_all x1 -> x2, blocking collectives: 12.7 us -> 34.5 us  [the longest x1 22.3 us: on_device(): far = lax.all_to_all(merged, 'z', 0, 0)]
    all_to_all x1 -> x0, waiting for transfers between devices: 12.1 us -> none  [on_device(): far = lax.all_to_all(merged, 'z', 0, 0)]
    all_to_all x1 -> x0, starting transfers between devices: 10 us -> none  [on_device(): far = lax.all_to_all(merged, 'z', 0, 0)]
    pallas_call x1, Pallas kernels: 4.77 us -> 1.04 us  [on_device(): pl.pallas_call(half_kernel, out_shape=(logits, logits), in_specs=[VMEM] *...]
    pallas_call x1, Pallas kernels: 2.92 us -> 0.25 us  [on_device(): pl.pallas_call(spread_kernel, out_shape=jax.ShapeDtypeStruct((ny * nx, gr...]
    unnamed x4 -> x14, local copies, waits for them, and re-layouts: 0.65 us -> 2.93 us
    pallas_call x1, Pallas kernels: 6.45 us -> 4.57 us  [on_device(): pl.pallas_call(stats_kernel, out_shape=(whole, whole, jax.ShapeDtypeStruc...]
    pallas_call x2, Pallas kernels: 7.46 us -> 5.94 us  [the longest x1 5.8 us: on_device(): pl.pallas_call(grad_kernel, out_shape=(jax.ShapeDtypeStruct((1, grp_rows)...]
  transfers between devices with their start and end apart: 2 -> 1, of which waited for: 2 -> 1; matrix products, arithmetic and copies ran while one was open for 0% -> 0% of each run, Pallas kernels for 3% -> 1%
where the time goes in v2:
time: 135 us; the launch traced here: 134 us
  blocking collectives  107 us (79%)
  Pallas kernels  11.8 us (9%)
  starting transfers between devices  8.54 us (6%)
  local copies, waits for them, and re-layouts  2.95 us (2%)
  waiting for transfers between devices  1.72 us (1%)
    all_to_all x1, blocking collectives, on_device(): own = lax.all_to_all(copies, ('y', 'x'), 0, 0).reshape(half, dt + ds)  43.6 us
    all_to_all x1, blocking collectives, on_device(): lax.all_to_all(jnp.broadcast_to(local, (nz,) + local.shape), 'z', 0, 0)  29.3 us
    all_to_all x1, blocking collectives, on_device(): far = lax.all_to_all(merged, 'z', 0, 0)  22.3 us
    all_to_all x1, blocking collectives, on_device(): near = lax.all_to_all(stats, ('y', 'x', 'c'), 0, 0)  12.2 us
    ppermute x1, starting transfers between devices, on_device(): other = lax.ppermute(own, 'c', [(0, 1), (1, 0)])  8.54 us
    pallas_call x1, Pallas kernels, on_device(): pl.pallas_call(grad_kernel, out_shape=(jax.ShapeDtypeStruct((1, grp_rows)...  5.8 us
    pallas_call x1, Pallas kernels, on_device(): pl.pallas_call(stats_kernel, out_shape=(whole, whole, jax.ShapeDtypeStruc...  4.57 us
    unnamed x14, local copies, waits for them, and re-layouts  2.93 us
  transfers between devices with their start and end apart: 1, of which 1 were waited for; matrix products, arithmetic and copies ran while one was open for 0% of the time, Pallas kernels for 1%

profile of v2, /device:TPU:1, one launch (start us, length us, event | category | flops | bytes accessed | tf_op | source)
XLA Modules:
  0.0 133.8 jit_solution(1169126363296289808)
XLA Ops:
  0.6 0.7 pad_maximum_fusion
  1.4 29.3 %all_to_all.20.gathered = bf16[16,16,416]{2,1,0:T(8,128)(2,1)S(1)} all-to-all(bf16[16,16,416]{2,1,0:T(8,128)(2,1)S(1)} %broadcast_in_dim.12), channel_id=1, replica_groups=mesh['y'=4,'x'=4,'c'=2,'z'=16] {'z'}, dimensions={0} | all-to-all | bytes 425984 | tf_op jit(solution)/shard_map/all_to_all | solution.py:165
  30.7 0.2 shard_map.95
  30.9 43.6 %all_to_all.21 = bf16[16,16,6656]{2,1,0:T(8,128)(2,1)S(1)} all-to-all(bf16[16,16,6656]{2,1,0:T(8,128)(2,1)S(1)} %shard_map.95), channel_id=1, replica_groups=mesh['y'=4,'x'=4,'c'=2,'z'=16] {'y','x'}, dimensions={0} | all-to-all | bytes 6815744 | tf_op jit(solution)/shard_map/all_to_all | solution.py:171
  74.5 8.5 %collective-permute-start = (bf16[256,6656]{1,0:T(8,128)(2,1)S(1)}, bf16[256,6656]{1,0:T(8,128)(2,1)}, u32[]{:S(2)}, u32[]{:S(2)}) collective-permute-start(bf16[256,6656]{1,0:T(8,128)(2,1)S(1)} %bitcast.8), channel_id=1, source_target_pairs={{0,16},{16,0},{1,17},{17,1},{2,18},{18,2},{3,19},{19,3},{4,20},{20... | collective-permute-start | bytes 10223624 | tf_op jit(solution)/shard_map/ppermute | solution.py:172
  83.1 0.1 pad_add_fusion.where
  83.1 0.0 copy-start
  83.1 1.6 %copy-done = bf16[4096,256]{1,0:T(8,128)(2,1)S(1)} copy-done((bf16[4096,256]{1,0:T(8,128)(2,1)S(1)}, bf16[4096,256]{1,0:T(8,128)(2,1)}, u32[]{:S(2)}) %copy-start) | copy-done | bytes 2097176
  84.7 0.0 copy-start.2
  84.7 1.3 copy-done.2
  86.0 0.0 copy-start.1
  86.1 0.0 copy-start.3
  86.1 0.0 copy-start.4
  86.1 1.0 shard_map.96
  87.1 1.7 %collective-permute-done.rows.other = bf16[256,6656]{1,0:T(8,128)(2,1)} collective-permute-done((bf16[256,6656]{1,0:T(8,128)(2,1)S(1)}, bf16[256,6656]{1,0:T(8,128)(2,1)}, u32[]{:S(2)}, u32[]{:S(2)}) %collective-permute-start) | collective-permute-done | bytes 3407904 | tf_op jit(solution)/shard_map/ppermute | solution.py:172
  88.8 0.0 copy-done.1
  88.8 0.0 copy-done.3
  88.8 0.0 copy-done.4
  88.8 0.0 copy-start.5
  88.8 0.0 copy-start.6
  88.8 4.6 %shard_map.97 = (f32[256,512]{1,0:T(8,128)S(1)}, f32[256,512]{1,0:T(8,128)S(1)}, f32[32,16,128]{2,1,0:T(8,128)S(1)}) custom-call(s32[3]{0:T(128)S(1)} %pad_add_fusion.where, bf16[256,6656]{1,0:T(8,128)(2,1)} %collective-permute-done.rows.other, bf16[2560,256]{1,0:T(8,128)(2,1)S(1)} %copy-done.2, bf16[4096,256]{1,0:T(8,128)(2,1)S(1)} %copy-done.1, ...), custom_call_target="tpu_custom_call" | custom-call | tf_op jit(solution)/shard_map/pallas_call | solution.py:180
  93.4 12.2 %all_to_all.22.parts = f32[32,16,128]{2,1,0:T(8,128)S(1)} all-to-all(f32[32,16,128]{2,1,0:T(8,128)S(1)} %get-tuple-element.11), channel_id=1, replica_groups=mesh['y'=4,'x'=4,'c'=2,'z'=16] {'y','x','c'}, dimensions={0} | all-to-all | bytes 524288 | tf_op jit(solution)/shard_map/all_to_all | solution.py:186
  105.6 0.1 shard_map.98
  105.8 22.3 %all_to_all.23.parts = f32[16,16,128]{2,1,0:T(8,128)S(1)} all-to-all(f32[16,16,128]{2,1,0:T(8,128)S(1)} %shard_map.98), channel_id=1, replica_groups=mesh['y'=4,'x'=4,'c'=2,'z'=16] {'z'}, dimensions={0} | all-to-all | bytes 262144 | tf_op jit(solution)/shard_map/all_to_all | solution.py:192
  128.0 0.0 copy-done.5
  128.0 0.0 copy-done.6
  128.0 5.8 %shard_map.99 = (f32[1,16]{1,0:T(1,128)}, bf16[2560,256]{1,0:T(8,128)(2,1)}) custom-call(s32[3]{0:T(128)S(1)} %pad_add_fusion.where, s32[32]{0:T(128)S(1)} %copy-done.6, f32[16,16,128]{2,1,0:T(8,128)S(1)} %all_to_all.23.parts, f32[256,512]{1,0:T(8,128)S(1)} %get-tuple-element.12.s_t, f32[256,512]{1,0:T(8,128)S(1)} %get-tuple-element.13.u_t, ...), custom_call_target="tpu_custom_call" | custom-call | tf_op jit(solution)/shard_map/pallas_call | solution.py:193
  (1 shorter events, 0.0 us)
Async XLA Ops:
  74.5 14.3 %collective-permute-start = (bf16[256,6656]{1,0:T(8,128)(2,1)S(1)}, bf16[256,6656]{1,0:T(8,128)(2,1)}, u32[]{:S(2)}, u32[]{:S(2)}) collective-permute-start(bf16[256,6656]{1,0:T(8,128)(2,1)S(1)} %bitcast.8), channel_id=1, source_target_pairs={{0,16},{16,0},{1,17},{17,1},{2,18},{18,2},{3,19},{19,3},{4,20},{20... | collective-permute-start | bytes 10223624 | tf_op jit(solution)/shard_map/ppermute | solution.py:172
  83.1 1.6 %copy-start = (bf16[4096,256]{1,0:T(8,128)(2,1)S(1)}, bf16[4096,256]{1,0:T(8,128)(2,1)}, u32[]{:S(2)}) copy-start(bf16[4096,256]{1,0:T(8,128)(2,1)} %head_t.3) | copy-start | bytes 6291460
  84.7 1.3 copy-start.2
  86.0 2.8 %copy-start.1 = (bf16[4096,256]{1,0:T(8,128)(2,1)S(1)}, bf16[4096,256]{1,0:T(8,128)(2,1)}, u32[]{:S(2)}) copy-start(bf16[4096,256]{1,0:T(8,128)(2,1)} %head_t.3) | copy-start | bytes 6291460
  86.1 2.8 %copy-start.3 = (s32[512]{0:T(512)S(1)}, s32[512]{0:T(512)}, u32[]{:S(2)}) copy-start(s32[512]{0:T(512)} %param.13) | copy-start | bytes 6148
  86.1 2.8 %copy-start.4 = (s32[512]{0:T(512)S(1)}, s32[512]{0:T(512)}, u32[]{:S(2)}) copy-start(s32[512]{0:T(512)} %param.14) | copy-start | bytes 6148
  88.8 39.2 %copy-start.5 = (s32[512]{0:T(512)S(1)}, s32[512]{0:T(512)}, u32[]{:S(2)}) copy-start(s32[512]{0:T(512)} %param.15) | copy-start | bytes 6148
  88.8 39.2 %copy-start.6 = (s32[32]{0:T(128)S(1)}, s32[32]{0:T(128)}, u32[]{:S(2)}) copy-start(s32[32]{0:T(128)} %lengths.1) | copy-start | bytes 388

commit v3 on v2

v3 whole, which is shorter than its diff:
```python
import jax
import jax.numpy as jnp
from jax import lax
from jax.experimental import pallas as pl
from jax.experimental.pallas import tpu as pltpu
from jax.sharding import Mesh, PartitionSpec as P

F32 = jnp.float32
BF16 = jnp.bfloat16
VMEM = pl.BlockSpec(memory_space=pltpu.VMEM)
SMEM = pl.BlockSpec(memory_space=pltpu.SMEM)
LIVE = 320
ROWS = 40
QT, QS = 64, 40


def grant(mib):
    return pltpu.CompilerParams(vmem_limit_bytes=mib * 1024 * 1024)


def dot(a, b, dims=((1,), (0,))):
    return lax.dot_general(a, b, (dims, ((), ())), preferred_element_type=F32)


def ranks(lengths, tokens):
    slot = lax.broadcasted_iota(jnp.int32, (1, tokens), 1)
    window, row = slot // 16, slot % 16
    rank = jnp.full((1, tokens), -1, jnp.int32)
    start = jnp.int32(0)
    for w in range(lengths.shape[0]):
        here = jnp.logical_and(window == w, row < lengths[w])
        rank = jnp.where(here, row + start, rank)
        start = start + lengths[w]
    return rank


def pick_kernel(where, lengths, near, route, out):
    chunk, quarter = where[3], where[4]
    tokens = route.shape[1]
    rows = near[...].reshape(tokens, near.shape[2])
    place = lax.broadcasted_iota(jnp.int32, (ROWS, tokens), 0) + chunk * ROWS
    pick_s = jnp.where(place == ranks(lengths, tokens), 1.0, 0.0).astype(BF16)
    order = lax.broadcasted_iota(jnp.int32, (tokens, tokens), 0)
    sent = jnp.where(order == route[...], 1.0, 0.0).astype(BF16)
    pick_t = dot(pick_s, sent).astype(BF16)
    teacher = dot(pick_t, rows[:, : 4 * QT])
    student = dot(pick_s, rows[:, 4 * QT :])
    part_t, part_s = teacher[:, :QT], student[:, :QS]
    for q in range(1, 4):
        part_t = jnp.where(quarter == q, teacher[:, QT * q : QT * q + QT], part_t)
        part_s = jnp.where(quarter == q, student[:, QS * q : QS * q + QS], part_s)
    block = jnp.concatenate([part_t, part_s], axis=1).astype(BF16)
    for i in range(out.shape[0]):
        out[i] = block


def spread_kernel(gathered, out):
    nz = gathered.shape[0]
    teacher = [gathered[z, :, :QT] for z in range(nz)]
    student = [gathered[z, :, QT:] for z in range(nz)]
    whole = jnp.concatenate(teacher + student, axis=1)
    for i in range(out.shape[0]):
        out[i] = whole


def logits_of(rows, head_s, head_t, core):
    dt = head_t.shape[1]
    s = sum(dot(rows[i, :, dt:], head_s[2 * core + i]) for i in range(2))
    u = sum(dot(rows[i, :, :dt], head_t[2 * core + i]) for i in range(2))
    return s, u


def half_kernel(where, rows, head_s, head_t, s_out, u_out):
    s_out[...], u_out[...] = logits_of(rows, head_s, head_t, where[0])


def stats_kernel(
    where, lengths, rows, head_s, head_t, s_own, u_own, ids, s_t_out, u_t_out, stats_out
):
    core, first_col = where[0], where[1]
    tokens = ids.shape[1]
    s, u = logits_of(rows, head_s, head_t, 1 - core)
    s_t = (s_own[...] + s).T
    u_t = (u_own[...] + u).T
    s_t_out[...] = s_t
    u_t_out[...] = u_t
    m_s = jnp.max(s_t, axis=0, keepdims=True)
    m_u = jnp.max(u_t, axis=0, keepdims=True)
    s_rel = s_t - m_s
    u_rel = u_t - m_u
    e_s = jnp.exp(s_rel)
    sum_s = jnp.sum(e_s, axis=0, keepdims=True)
    sum_u = jnp.sum(jnp.exp(u_rel), axis=0, keepdims=True)
    mean = jnp.sum(e_s * (s_rel - u_rel), axis=0, keepdims=True) / sum_s
    log_s = jnp.log(sum_s)
    log_u = jnp.log(sum_u)
    place = lax.broadcasted_iota(jnp.int32, (LIVE, tokens), 0)
    live = jnp.where(place == ranks(lengths, tokens), 1.0, 0.0).astype(BF16)
    all_ids = ids[...]
    digits = [all_ids % 64, all_ids // 64 % 64, all_ids // 4096]
    digits = jnp.concatenate([d.astype(F32) for d in digits] + [jnp.zeros((5, tokens), F32)], axis=0)
    digits = dot(digits.astype(BF16), live, ((1,), (1,))).astype(jnp.int32)
    wanted = digits[0:1] + 64 * digits[1:2] + 4096 * digits[2:3]
    column = lax.broadcasted_iota(jnp.int32, s_t.shape, 0)
    hit = column == wanted - first_col
    apart = jnp.sum(jnp.where(hit, u_t - s_t, 0.0), axis=0, keepdims=True)
    values = (m_s + log_s, m_u + log_u, mean - log_s + log_u, apart)
    lines = [v[:, 128 * j : 128 * j + 128] for v in values for j in range(2)]
    ends = jnp.concatenate([v[:, 256:LIVE] for v in values], axis=1)
    block = jnp.concatenate(lines + [ends[:, :128], ends[:, 128:], jnp.zeros((6, 128), F32)], axis=0)
    for i in range(stats_out.shape[0]):
        stats_out[i] = block


def merge(lse_s, lse_u, kl, apart):
    m_s = jnp.max(lse_s, axis=0)
    m_u = jnp.max(lse_u, axis=0)
    all_s = m_s + jnp.log(jnp.sum(jnp.exp(lse_s - m_s), axis=0))
    all_u = m_u + jnp.log(jnp.sum(jnp.exp(lse_u - m_u), axis=0))
    share = jnp.exp(lse_s - all_s)
    whole = jnp.sum(share * (kl + (lse_s - all_s) - (lse_u - all_u)), axis=0)
    return all_s, all_u, whole, jnp.sum(apart, axis=0)


def merge_lines(parts):
    main = merge(*(parts[:, 2 * k : 2 * k + 2] for k in range(4)))
    first, second = parts[:, 8:9], parts[:, 9:10]
    ends = merge(first[:, :, :64], first[:, :, 64:], second[:, :, :64], second[:, :, 64:])
    return main, ends


def merge_kernel(parts, out):
    main, ends = merge_lines(parts[...])
    tail = [jnp.concatenate(ends[:2], axis=1), jnp.concatenate(ends[2:], axis=1)]
    block = jnp.concatenate(list(main) + tail + [jnp.zeros((6, 128), F32)], axis=0)
    for i in range(out.shape[0]):
        out[i] = block


def grad_kernel(where, lengths, parts, s_t, u_t, flags, own, other, kl_out, grad_out):
    core, group = where[0], where[2]
    tokens = flags.shape[1]
    nz = grad_out.shape[0]
    dt = own.shape[2] - nz * QS
    main, ends = merge_lines(parts[...])
    lse_s, lse_u, kl, apart = [
        jnp.concatenate([m[0:1], m[1:2], e], axis=1) for m, e in zip(main, ends)
    ]
    place = lax.broadcasted_iota(jnp.int32, (LIVE, tokens), 0)
    live = jnp.where(place == ranks(lengths, tokens), 1.0, 0.0).astype(BF16)
    marks = jnp.broadcast_to(flags[...], (8, tokens)).astype(F32).astype(BF16)
    mark = dot(marks, live, ((1,), (1,)))[0:1]
    mixed = 1.0 / (0.2 * jnp.exp(apart - lse_u + lse_s) + 0.8)
    weight = jnp.where(mark > 0.5, mixed, jnp.ones_like(mixed))
    log_s = s_t[...] - lse_s
    gap = log_s - (u_t[...] - lse_u)
    d_t = (weight * jnp.exp(log_s) * (gap - kl)).astype(BF16)
    for half, rows in ((core, own), (1 - core, other)):
        for i in range(2):
            total = dot(d_t, rows[i, :, dt:]).T
            for z in range(nz):
                grad_out[z, 2 * half + i] = total[QS * z : QS * z + QS].astype(BF16)
    start = jnp.int32(0)
    for w in range(lengths.shape[0]):
        start = start + jnp.where(w < group, lengths[w], 0)
    row = lax.broadcasted_iota(jnp.int32, (16, LIVE), 0)
    column = lax.broadcasted_iota(jnp.int32, (16, LIVE), 1)
    mine = jnp.logical_and(column == row + start, row < lengths[group])
    mine = jnp.sum(jnp.where(mine, kl, 0.0), axis=1, keepdims=True)
    kl_out[...] = jnp.broadcast_to(mine, (16, 128)).T[0:1]


def on_device(
    student_hidden, teacher_rows, student_head, teacher_head, lengths, route, sampled_ids, mix_flags
):
    nz = lax.axis_size("z")
    core = lax.axis_index("c")
    x_hi, x_lo = lax.axis_index("xh"), lax.axis_index("xl")
    group = ((lax.axis_index("y") * 2 + x_hi) * 2 + x_lo) * 2 + core
    grp_rows = student_hidden.shape[0]
    ds, vocab_dev = student_head.shape
    dt = teacher_head.shape[0]
    quarter = (ds + dt) // 4
    first_col = (group * nz + lax.axis_index("z")) * vocab_dev
    where = [core, first_col, group, lax.axis_index("y") * 2 + x_hi, 2 * core + x_lo]
    where = jnp.stack(where).astype(jnp.int32)
    tok = ("y", "xh", "xl", "c")

    local = jnp.concatenate([teacher_rows, student_hidden], axis=1)
    near = lax.all_to_all(jnp.broadcast_to(local, (32,) + local.shape), tok, 0, 0)
    picked = pl.pallas_call(
        pick_kernel,
        out_shape=jax.ShapeDtypeStruct((nz, ROWS, QT + QS), BF16),
        in_specs=[SMEM] * 2 + [VMEM] * 2, out_specs=VMEM, compiler_params=grant(8),
    )(where, lengths, near, route[None])
    gathered = lax.all_to_all(picked, "z", 0, 0)
    copies = pl.pallas_call(
        spread_kernel,
        out_shape=jax.ShapeDtypeStruct((16, ROWS, quarter), BF16),
        in_specs=[VMEM], out_specs=VMEM, compiler_params=grant(8),
    )(gathered)
    own = lax.all_to_all(copies, ("xl", "y", "xh"), 0, 0).reshape(2, LIVE, quarter)
    other = lax.ppermute(own, "c", [(0, 1), (1, 0)])
    head_s = student_head.reshape(nz, 4, QS, vocab_dev).transpose(1, 0, 2, 3)
    head_s = head_s.reshape(4, ds // 4, vocab_dev)
    head_t = teacher_head.reshape(nz, 4, QT, vocab_dev).transpose(1, 0, 2, 3)
    head_t = head_t.reshape(4, dt // 4, vocab_dev)
    logits = jax.ShapeDtypeStruct((LIVE, vocab_dev), F32)
    s_own, u_own = pl.pallas_call(
        half_kernel, out_shape=(logits, logits),
        in_specs=[SMEM] + [VMEM] * 3, out_specs=(VMEM, VMEM), compiler_params=grant(8),
    )(where, own, head_s, head_t)
    whole = jax.ShapeDtypeStruct((vocab_dev, LIVE), F32)
    s_t, u_t, stats = pl.pallas_call(
        stats_kernel,
        out_shape=(whole, whole, jax.ShapeDtypeStruct((32, 16, 128), F32)),
        in_specs=[SMEM] * 2 + [VMEM] * 6, out_specs=(VMEM,) * 3, compiler_params=grant(8),
    )(where, lengths, other, head_s, head_t, s_own, u_own, sampled_ids[None])
    parts = lax.all_to_all(stats, tok, 0, 0)
    merged = pl.pallas_call(
        merge_kernel,
        out_shape=jax.ShapeDtypeStruct((nz, 16, 128), F32),
        in_specs=[VMEM], out_specs=VMEM, compiler_params=grant(4),
    )(parts)
    parts = lax.all_to_all(merged, "z", 0, 0)
    kl_rows, head_grad = pl.pallas_call(
        grad_kernel,
        out_shape=(
            jax.ShapeDtypeStruct((1, grp_rows), F32),
            jax.ShapeDtypeStruct((nz, 4, QS, vocab_dev), BF16),
        ),
        in_specs=[SMEM] * 2 + [VMEM] * 6, out_specs=(VMEM,) * 2, compiler_params=grant(8),
    )(where, lengths, parts, s_t, u_t, mix_flags[None], own, other)
    return kl_rows[0], head_grad.reshape(ds, vocab_dev)


def solution(mesh):
    axes = ("y", "xh", "xl", "c", "z")
    fine = Mesh(mesh.devices.reshape(4, 2, 2, 2, 16), axes)
    tok = axes[:4]
    in_specs = (P(tok, "z"), P(tok, "z"), P(None, axes), P(None, axes), P(), P(), P(), P())
    out_specs = (P(tok), P(None, axes))
    return jax.shard_map(
        on_device, mesh=fine, in_specs=in_specs, out_specs=out_specs, check_vma=False
    )
```

time: 135 us -> 130 us (0.963)
  blocking collectives: 107 us -> 86.3 us
  waiting for transfers between devices: 1.72 us -> 13.6 us
  starting transfers between devices: 8.54 us -> 16.5 us
  Pallas kernels: 11.8 us -> 7.73 us
    all_to_all x4, blocking collectives: 107 us -> 86.3 us  [the longest x1 30.4 us: on_device(): lax.all_to_all(copies, ('xl', 'y', 'xh'), 0, 0).reshape(2, LIVE, quarter)]
    all_to_all x0 -> x1, waiting for transfers between devices: none -> 11.4 us  [on_device(): lax.all_to_all(jnp.broadcast_to(local, (32,) + local.shape), tok, 0, 0)]
    all_to_all x0 -> x1, starting transfers between devices: none -> 10.4 us  [on_device(): lax.all_to_all(jnp.broadcast_to(local, (32,) + local.shape), tok, 0, 0)]
    pallas_call x1, Pallas kernels: 4.57 us -> 1.72 us  [on_device(): pl.pallas_call(stats_kernel, out_shape=(whole, whole, jax.ShapeDtypeStruc...]
    pallas_call x1, Pallas kernels: 5.8 us -> 2.97 us  [on_device(): pl.pallas_call(grad_kernel, out_shape=(jax.ShapeDtypeStruct((1, grp_rows)...]
    ppermute x1, starting transfers between devices: 8.54 us -> 6.1 us  [on_device(): other = lax.ppermute(own, 'c', [(0, 1), (1, 0)])]
    pallas_call x3 -> x4, Pallas kernels: 1.43 us -> 3.04 us  [the longest x1 1.3 us: on_device(): pl.pallas_call(half_kernel, out_shape=(logits, logits), in_specs=[SMEM] +...]
    unnamed x14, local copies, waits for them, and re-layouts: 2.93 us -> 1.36 us
  transfers between devices with their start and end apart: 1 -> 2, of which waited for: 1 -> 2; matrix products, arithmetic and copies ran while one was open for 0% -> 0% of each run, Pallas kernels for 1% -> 1%
where the time goes in v3:
time: 130 us; the launch traced here: 128 us
  blocking collectives  86.3 us (66%)
  starting transfers between devices  16.5 us (13%)
  waiting for transfers between devices  13.6 us (10%)
  Pallas kernels  7.73 us (6%)
  local copies, waits for them, and re-layouts  2.62 us (2%)
    all_to_all x1, blocking collectives, on_device(): lax.all_to_all(copies, ('xl', 'y', 'xh'), 0, 0).reshape(2, LIVE, quarter)  30.4 us
    all_to_all x1, blocking collectives, on_device(): gathered = lax.all_to_all(picked, 'z', 0, 0)  25.1 us
    all_to_all x1, blocking collectives, on_device(): parts = lax.all_to_all(merged, 'z', 0, 0)  18.6 us
    all_to_all x1, blocking collectives, on_device(): parts = lax.all_to_all(stats, tok, 0, 0)  12.3 us
    all_to_all x1, waiting for transfers between devices, on_device(): lax.all_to_all(jnp.broadcast_to(local, (32,) + local.shape), tok, 0, 0)  11.4 us
    all_to_all x1, starting transfers between devices, on_device(): lax.all_to_all(jnp.broadcast_to(local, (32,) + local.shape), tok, 0, 0)  10.4 us
    ppermute x1, starting transfers between devices, on_device(): other = lax.ppermute(own, 'c', [(0, 1), (1, 0)])  6.1 us
    pallas_call x1, Pallas kernels, on_device(): pl.pallas_call(grad_kernel, out_shape=(jax.ShapeDtypeStruct((1, grp_rows)...  2.97 us
  transfers between devices with their start and end apart: 2, of which 2 were waited for; matrix products, arithmetic and copies ran while one was open for 0% of the time, Pallas kernels for 1%

profile of v3, /device:TPU:1, one launch (start us, length us, event | category | flops | bytes accessed | tf_op | source)
XLA Modules:
  0.0 128.2 jit_solution(14224605635725685551)
XLA Ops:
  0.6 0.7 pad_maximum_fusion
  1.4 0.9 broadcast_in_dim.12
  2.2 10.4 %all-to-all-start = ((bf16[32,16,416]{2,1,0:T(8,128)(2,1)}), bf16[32,16,416]{2,1,0:T(8,128)(2,1)S(1)}, u32[]{:S(2)}, u32[]{:S(2)}) async-start(bf16[32,16,416]{2,1,0:T(8,128)(2,1)} %broadcast_in_dim.12), calls=%async_computation | async-start | bytes 1048576 | tf_op jit(solution)/shard_map/all_to_all | solution.py:190
  12.6 0.1 stack.23.where
  12.7 11.4 %all-to-all-done.near = bf16[32,16,416]{2,1,0:T(8,128)(2,1)S(1)} async-done(((bf16[32,16,416]{2,1,0:T(8,128)(2,1)}), bf16[32,16,416]{2,1,0:T(8,128)(2,1)S(1)}, u32[]{:S(2)}, u32[]{:S(2)}) %all-to-all-start) | async-done | bytes 426016 | tf_op jit(solution)/shard_map/all_to_all | solution.py:190
  24.1 0.0 copy-start
  24.1 0.7 copy-done
  24.8 0.0 copy-start.2
  24.8 0.7 copy-done.2
  25.5 1.2 shard_map.95
  26.7 25.1 %all_to_all.25.gathered = bf16[16,40,104]{2,1,0:T(8,128)(2,1)S(1)} all-to-all(bf16[16,40,104]{2,1,0:T(8,128)(2,1)S(1)} %shard_map.95), channel_id=1, replica_groups=mesh['y'=4,'xh'=2,'xl'=2,'c'=2,'z'=16] {'z'}, dimensions={0} | all-to-all | bytes 266240 | tf_op jit(solution)/shard_map/all_to_all | solution.py:196
  51.8 0.2 shard_map.96
  52.1 0.0 copy-start.6
  52.1 30.4 %all_to_all.26 = bf16[16,40,1664]{2,1,0:T(8,128)(2,1)S(1)} all-to-all(bf16[16,40,1664]{2,1,0:T(8,128)(2,1)S(1)} %shard_map.96), channel_id=1, replica_groups=mesh['y'=4,'xh'=2,'xl'=2,'c'=2,'z'=16] {'xl','y','xh'}, dimensions={0} | all-to-all | bytes 4259840 | tf_op jit(solution)/shard_map/all_to_all | solution.py:202
  82.4 0.0 copy-start.5
  82.4 6.1 %collective-permute-start = (bf16[2,320,1664]{2,1,0:T(8,128)(2,1)S(1)}, bf16[2,320,1664]{2,1,0:T(8,128)(2,1)S(1)}, u32[]{:S(2)}, u32[]{:S(2)}) collective-permute-start(bf16[2,320,1664]{2,1,0:T(8,128)(2,1)S(1)} %bitcast.19), channel_id=1, source_target_pairs={{0,16},{16,0},{1,17},{17,1},{2,18},{18,2},{3,19},{19,3},{4,20},{20... | collective-permute-start | bytes 6389768 | tf_op jit(solution)/shard_map/ppermute | solution.py:203
  88.5 0.0 copy-done.6
  88.5 0.1 copy.10
  88.6 0.0 copy-done.5
  88.6 0.2 copy.11
  88.9 0.0 copy-start.1
  88.9 0.0 copy-start.3
  88.9 1.3 %shard_map.97 = (f32[320,256]{1,0:T(8,128)S(1)}, f32[320,256]{1,0:T(8,128)S(1)}) custom-call(s32[5]{0:T(128)S(1)} %stack.23.where, bf16[2,320,1664]{2,1,0:T(8,128)(2,1)S(1)} %bitcast.20, bf16[4,640,256]{2,1,0:T(8,128)(2,1)S(1)} %bitcast.24, bf16[4,1024,256]{2,1,0:T(8,128)(2,1)S(1)} %bitcast.22), custom_call_target="tpu_custom_call" | custom-call | tf_op jit(solution)/shard_map/pallas_call | solution.py:209
  90.2 2.1 %collective-permute-done.rows.other = bf16[2,320,1664]{2,1,0:T(8,128)(2,1)S(1)} collective-permute-done((bf16[2,320,1664]{2,1,0:T(8,128)(2,1)S(1)}, bf16[2,320,1664]{2,1,0:T(8,128)(2,1)S(1)}, u32[]{:S(2)}, u32[]{:S(2)}) %collective-permute-start) | collective-permute-done | bytes 2129952 | tf_op jit(solution)/shard_map/ppermute | solution.py:203
  92.3 0.0 copy-done.1
  92.3 0.0 copy-done.3
  92.3 1.7 %shard_map.98 = (f32[256,320]{1,0:T(8,128)S(1)}, f32[256,320]{1,0:T(8,128)S(1)}, f32[32,16,128]{2,1,0:T(8,128)S(1)}) custom-call(s32[5]{0:T(128)S(1)} %stack.23.where, s32[32]{0:T(128)S(1)} %copy-done.1, bf16[2,320,1664]{2,1,0:T(8,128)(2,1)S(1)} %collective-permute-done.rows.other, bf16[4,640,256]{2,1,0:T(8,128)(2,1)S(1)} %bitcast.25, ...), custom_call_target="tpu_custom_call" | custom-call | tf_op jit(solution)/shard_map/pallas_call | solution.py:214
  94.1 12.3 %all_to_all.27.parts = f32[32,16,128]{2,1,0:T(8,128)S(1)} all-to-all(f32[32,16,128]{2,1,0:T(8,128)S(1)} %get-tuple-element.11), channel_id=1, replica_groups=mesh['y'=4,'xh'=2,'xl'=2,'c'=2,'z'=16] {'y','xh','xl','c'}, dimensions={0} | all-to-all | bytes 524288 | tf_op jit(solution)/shard_map/all_to_all | solution.py:219
  106.4 0.3 shard_map.99
  106.6 18.6 %all_to_all.28.parts = f32[16,16,128]{2,1,0:T(8,128)S(1)} all-to-all(f32[16,16,128]{2,1,0:T(8,128)S(1)} %shard_map.99), channel_id=1, replica_groups=mesh['y'=4,'xh'=2,'xl'=2,'c'=2,'z'=16] {'z'}, dimensions={0} | all-to-all | bytes 262144 | tf_op jit(solution)/shard_map/all_to_all | solution.py:225
  125.2 0.0 copy-done.4
  125.2 3.0 %shard_map.100 = (f32[1,16]{1,0:T(1,128)}, bf16[16,4,40,256]{3,2,1,0:T(8,128)(2,1)}) custom-call(s32[5]{0:T(128)S(1)} %stack.23.where, s32[32]{0:T(128)S(1)} %copy-done.1, f32[16,16,128]{2,1,0:T(8,128)S(1)} %all_to_all.28.parts, f32[256,320]{1,0:T(8,128)S(1)} %get-tuple-element.12.s_t, f32[256,320]{1,0:T(8,128)S(1)} %get-tuple-element.13.u_t, ...), custom_call_target="tpu_custom_call" | custom-call | tf_op jit(solution)/shard_map/pallas_call | solution.py:226
  (1 shorter events, 0.0 us)
Async XLA Ops:
  2.2 21.9 %all-to-all-start = ((bf16[32,16,416]{2,1,0:T(8,128)(2,1)}), bf16[32,16,416]{2,1,0:T(8,128)(2,1)S(1)}, u32[]{:S(2)}, u32[]{:S(2)}) async-start(bf16[32,16,416]{2,1,0:T(8,128)(2,1)} %broadcast_in_dim.12), calls=%async_computation | async-start | bytes 1048576 | tf_op jit(solution)/shard_map/all_to_all | solution.py:190
  24.1 0.7 copy-start
  24.8 0.7 copy-start.2
  52.1 36.5 %copy-start.6 = (bf16[2560,256]{1,0:T(8,128)(2,1)S(1)}, bf16[2560,256]{1,0:T(8,128)(2,1)}, u32[]{:S(2)}) copy-start(bf16[2560,256]{1,0:T(8,128)(2,1)} %param.10) | copy-start | bytes 3932164
  82.4 6.2 %copy-start.5 = (bf16[4096,256]{1,0:T(8,128)(2,1)S(1)}, bf16[4096,256]{1,0:T(8,128)(2,1)}, u32[]{:S(2)}) copy-start(bf16[4096,256]{1,0:T(8,128)(2,1)} %param.11) | copy-start | bytes 6291460
  82.4 9.9 %collective-permute-start = (bf16[2,320,1664]{2,1,0:T(8,128)(2,1)S(1)}, bf16[2,320,1664]{2,1,0:T(8,128)(2,1)S(1)}, u32[]{:S(2)}, u32[]{:S(2)}) collective-permute-start(bf16[2,320,1664]{2,1,0:T(8,128)(2,1)S(1)} %bitcast.19), channel_id=1, source_target_pairs={{0,16},{16,0},{1,17},{17,1},{2,18},{18,2},{3,19},{19,3},{4,20},{20... | collective-permute-start | bytes 6389768 | tf_op jit(solution)/shard_map/ppermute | solution.py:203
  88.9 3.5 %copy-start.1 = (s32[32]{0:T(128)S(1)}, s32[32]{0:T(128)}, u32[]{:S(2)}) copy-start(s32[32]{0:T(128)} %lengths.5) | copy-start | bytes 388
  88.9 3.4 %copy-start.3 = (s32[512]{0:T(512)S(1)}, s32[512]{0:T(512)}, u32[]{:S(2)}) copy-start(s32[512]{0:T(512)} %param.14) | copy-start | bytes 6148
  92.3 32.9 %copy-start.4 = (s32[512]{0:T(512)S(1)}, s32[512]{0:T(512)}, u32[]{:S(2)}) copy-start(s32[512]{0:T(512)} %param.15) | copy-start | bytes 6148

commit v4 on v3

v4 whole, which is shorter than its diff:
```python
import jax
import jax.numpy as jnp
from jax import lax
from jax.experimental import pallas as pl
from jax.experimental.pallas import tpu as pltpu
from jax.sharding import Mesh, PartitionSpec as P

F32 = jnp.float32
BF16 = jnp.bfloat16
VMEM = pl.BlockSpec(memory_space=pltpu.VMEM)
SMEM = pl.BlockSpec(memory_space=pltpu.SMEM)
LIVE = 320
ROWS = 40
QT, QS = 64, 40


def grant(mib):
    return pltpu.CompilerParams(vmem_limit_bytes=mib * 1024 * 1024)


def dot(a, b, dims=((1,), (0,))):
    return lax.dot_general(a, b, (dims, ((), ())), preferred_element_type=F32)


def ranks(table, tokens):
    slot = lax.broadcasted_iota(jnp.int32, (1, tokens), 1)
    window, row = slot // 16, slot % 16
    rank = jnp.full((1, tokens), -1, jnp.int32)
    start = jnp.int32(0)
    for w in range(table.shape[0] - 5):
        here = jnp.logical_and(window == w, row < table[5 + w])
        rank = jnp.where(here, row + start, rank)
        start = start + table[5 + w]
    return rank


def quarter_kernel(teacher_in, student_in, out, teacher, student, arrived):
    loads = [
        pltpu.make_async_copy(teacher_in, teacher, arrived.at[0]),
        pltpu.make_async_copy(student_in, student, arrived.at[1]),
    ]
    for load in loads:
        load.start()
    for load in loads:
        load.wait()
    blocks = []
    for q in range(4):
        part = [teacher[:, QT * q : QT * q + QT], student[:, QS * q : QS * q + QS]]
        blocks.append(jnp.concatenate(part, axis=1))
    for i in range(out.shape[0]):
        out[i] = blocks[2 * (i % 2) + i // 2 % 2]


def index_kernel(table, rows, pick_out, wanted_out, mark_out):
    chunk = table[3]
    tokens = rows.shape[1]
    rank = ranks(table, tokens)
    route, ids, flags = rows[0:1], rows[1:2], rows[2:3]
    place = lax.broadcasted_iota(jnp.int32, (ROWS, tokens), 0) + chunk * ROWS
    pick_s = jnp.where(place == rank, 1.0, 0.0).astype(BF16)
    order = lax.broadcasted_iota(jnp.int32, (tokens, tokens), 0)
    sent = jnp.where(order == route, 1.0, 0.0).astype(BF16)
    pick_out[0] = pick_s
    pick_out[1] = dot(pick_s, sent).astype(BF16)
    place = lax.broadcasted_iota(jnp.int32, (LIVE, tokens), 0)
    live = jnp.where(place == rank, 1.0, 0.0).astype(BF16)
    digits = [d.astype(F32) for d in (ids % 64, ids // 64 % 64, ids // 4096, flags)]
    digits = jnp.concatenate(digits + [jnp.zeros((4, tokens), F32)], axis=0)
    digits = dot(digits.astype(BF16), live, ((1,), (1,))).astype(jnp.int32)
    wanted_out[...] = digits[0:1] + 64 * digits[1:2] + 4096 * digits[2:3]
    mark_out[...] = digits[3:4]


def pick_kernel(near, pick, out):
    rows = near[...].reshape(near.shape[0] * near.shape[1], near.shape[2])
    block = jnp.concatenate([dot(pick[1], rows[:, :QT]), dot(pick[0], rows[:, QT:])], axis=1)
    block = block.astype(BF16)
    for i in range(out.shape[0]):
        out[i] = block


def spread_kernel(gathered, out):
    nz = gathered.shape[0]
    teacher = [gathered[z, :, :QT] for z in range(nz)]
    student = [gathered[z, :, QT:] for z in range(nz)]
    whole = jnp.concatenate(teacher + student, axis=1)
    for i in range(out.shape[0]):
        out[i] = whole


def logits_of(rows, head_s, head_t, core):
    dt = head_t.shape[1]
    s = sum(dot(rows[i, :, dt:], head_s[2 * core + i]) for i in range(2))
    u = sum(dot(rows[i, :, :dt], head_t[2 * core + i]) for i in range(2))
    return s, u


def half_kernel(where, rows, head_s, head_t, s_out, u_out):
    s_out[...], u_out[...] = logits_of(rows, head_s, head_t, where[0])


def stats_kernel(
    where, rows, head_s, head_t, s_own, u_own, wanted, s_t_out, u_t_out, stats_out
):
    core, first_col = where[0], where[1]
    s, u = logits_of(rows, head_s, head_t, 1 - core)
    s_t = (s_own[...] + s).T
    u_t = (u_own[...] + u).T
    s_t_out[...] = s_t
    u_t_out[...] = u_t
    m_s = jnp.max(s_t, axis=0, keepdims=True)
    m_u = jnp.max(u_t, axis=0, keepdims=True)
    s_rel = s_t - m_s
    u_rel = u_t - m_u
    e_s = jnp.exp(s_rel)
    sum_s = jnp.sum(e_s, axis=0, keepdims=True)
    sum_u = jnp.sum(jnp.exp(u_rel), axis=0, keepdims=True)
    mean = jnp.sum(e_s * (s_rel - u_rel), axis=0, keepdims=True) / sum_s
    log_s = jnp.log(sum_s)
    log_u = jnp.log(sum_u)
    column = lax.broadcasted_iota(jnp.int32, s_t.shape, 0)
    hit = column == wanted[...] - first_col
    apart = jnp.sum(jnp.where(hit, u_t - s_t, 0.0), axis=0, keepdims=True)
    block = jnp.concatenate([m_s + log_s, m_u + log_u, mean - log_s + log_u, apart], axis=1)
    for i in range(stats_out.shape[0]):
        stats_out[i] = block


def merge(parts):
    parts = parts[:, 0, :]
    lse_s, lse_u, kl, apart = [parts[:, LIVE * k : LIVE * k + LIVE] for k in range(4)]
    m_s = jnp.max(lse_s, axis=0, keepdims=True)
    m_u = jnp.max(lse_u, axis=0, keepdims=True)
    all_s = m_s + jnp.log(jnp.sum(jnp.exp(lse_s - m_s), axis=0, keepdims=True))
    all_u = m_u + jnp.log(jnp.sum(jnp.exp(lse_u - m_u), axis=0, keepdims=True))
    share = jnp.exp(lse_s - all_s)
    whole = share * (kl + (lse_s - all_s) - (lse_u - all_u))
    whole = jnp.sum(whole, axis=0, keepdims=True)
    return all_s, all_u, whole, jnp.sum(apart, axis=0, keepdims=True)


def merge_kernel(parts, out):
    block = jnp.concatenate(merge(parts[...]), axis=1)
    for i in range(out.shape[0]):
        out[i] = block


def grad_kernel(table, parts, s_t, u_t, mark, own, other, kl_out, grad_out):
    core, group = table[0], table[2]
    nz = grad_out.shape[0]
    dt = own.shape[2] - nz * QS
    lse_s, lse_u, kl, apart = merge(parts[...])
    mixed = 1.0 / (0.2 * jnp.exp(apart - lse_u + lse_s) + 0.8)
    weight = jnp.where(mark[...] == 1, mixed, jnp.ones_like(mixed))
    log_s = s_t[...] - lse_s
    gap = log_s - (u_t[...] - lse_u)
    d_t = (weight * jnp.exp(log_s) * (gap - kl)).astype(BF16)
    for half, rows in ((core, own), (1 - core, other)):
        for i in range(2):
            total = dot(d_t, rows[i, :, dt:]).T
            for z in range(nz):
                grad_out[z, 2 * half + i] = total[QS * z : QS * z + QS].astype(BF16)
    start = jnp.int32(0)
    for w in range(table.shape[0] - 5):
        start = start + jnp.where(w < group, table[5 + w], 0)
    row = lax.broadcasted_iota(jnp.int32, (16, LIVE), 0)
    column = lax.broadcasted_iota(jnp.int32, (16, LIVE), 1)
    mine = jnp.logical_and(column == row + start, row < table[5 + group])
    mine = jnp.sum(jnp.where(mine, kl, 0.0), axis=1, keepdims=True)
    kl_out[...] = jnp.broadcast_to(mine, (16, 128)).T[0:1]


def on_device(
    student_hidden, teacher_rows, student_head, teacher_head, lengths, route, sampled_ids, mix_flags
):
    nz = lax.axis_size("z")
    core = lax.axis_index("c")
    x_hi, x_lo = lax.axis_index("xh"), lax.axis_index("xl")
    group = ((lax.axis_index("y") * 2 + x_hi) * 2 + x_lo) * 2 + core
    grp_rows = student_hidden.shape[0]
    ds, vocab_dev = student_head.shape
    dt = teacher_head.shape[0]
    quarter = (ds + dt) // 4
    first_col = (group * nz + lax.axis_index("z")) * vocab_dev
    place = jnp.stack([core, first_col, group, lax.axis_index("y") * 2 + x_hi, x_lo])
    table = jnp.concatenate([place.astype(jnp.int32), lengths])
    rows = jnp.stack([route, sampled_ids, mix_flags])
    tok = ("y", "xh", "xl", "c")

    quarters = pl.pallas_call(
        quarter_kernel,
        out_shape=jax.ShapeDtypeStruct((32, grp_rows, QT + QS), BF16),
        in_specs=[pl.BlockSpec(memory_space=pltpu.HBM)] * 2, out_specs=VMEM,
        scratch_shapes=[
            pltpu.VMEM(teacher_rows.shape, BF16), pltpu.VMEM(student_hidden.shape, BF16),
            pltpu.SemaphoreType.DMA((2,)),
        ],
        compiler_params=grant(4),
    )(teacher_rows, student_hidden)
    near = lax.all_to_all(quarters, tok, 0, 0)
    per_row = jax.ShapeDtypeStruct((1, LIVE), jnp.int32)
    pick, wanted, mark = pl.pallas_call(
        index_kernel,
        out_shape=(jax.ShapeDtypeStruct((2, ROWS, route.shape[0]), BF16), per_row, per_row),
        in_specs=[SMEM, VMEM], out_specs=(VMEM,) * 3, compiler_params=grant(6),
    )(table, rows)
    picked = pl.pallas_call(
        pick_kernel,
        out_shape=jax.ShapeDtypeStruct((nz, ROWS, QT + QS), BF16),
        in_specs=[VMEM] * 2, out_specs=VMEM, compiler_params=grant(4),
    )(near, pick)
    gathered = lax.all_to_all(picked, "z", 0, 0)
    copies = pl.pallas_call(
        spread_kernel,
        out_shape=jax.ShapeDtypeStruct((16, ROWS, quarter), BF16),
        in_specs=[VMEM], out_specs=VMEM, compiler_params=grant(8),
    )(gathered)
    own = lax.all_to_all(copies, ("xl", "y", "xh"), 0, 0).reshape(2, LIVE, quarter)
    other = lax.ppermute(own, "c", [(0, 1), (1, 0)])
    head_s = student_head.reshape(nz, 4, QS, vocab_dev).transpose(1, 0, 2, 3)
    head_s = head_s.reshape(4, ds // 4, vocab_dev)
    head_t = teacher_head.reshape(nz, 4, QT, vocab_dev).transpose(1, 0, 2, 3)
    head_t = head_t.reshape(4, dt // 4, vocab_dev)
    logits = jax.ShapeDtypeStruct((LIVE, vocab_dev), F32)
    s_own, u_own = pl.pallas_call(
        half_kernel, out_shape=(logits, logits),
        in_specs=[SMEM] + [VMEM] * 3, out_specs=(VMEM, VMEM), compiler_params=grant(8),
    )(table, own, head_s, head_t)
    whole = jax.ShapeDtypeStruct((vocab_dev, LIVE), F32)
    s_t, u_t, stats = pl.pallas_call(
        stats_kernel,
        out_shape=(whole, whole, jax.ShapeDtypeStruct((32, 1, 4 * LIVE), F32)),
        in_specs=[SMEM] + [VMEM] * 6, out_specs=(VMEM,) * 3, compiler_params=grant(8),
    )(table, other, head_s, head_t, s_own, u_own, wanted)
    parts = lax.all_to_all(stats, tok, 0, 0)
    merged = pl.pallas_call(
        merge_kernel,
        out_shape=jax.ShapeDtypeStruct((nz, 1, 4 * LIVE), F32),
        in_specs=[VMEM], out_specs=VMEM, compiler_params=grant(4),
    )(parts)
    parts = lax.all_to_all(merged, "z", 0, 0)
    kl_rows, head_grad = pl.pallas_call(
        grad_kernel,
        out_shape=(
            jax.ShapeDtypeStruct((1, grp_rows), F32),
            jax.ShapeDtypeStruct((nz, 4, QS, vocab_dev), BF16),
        ),
        in_specs=[SMEM] + [VMEM] * 6, out_specs=(VMEM,) * 2, compiler_params=grant(8),
    )(table, parts, s_t, u_t, mark, own, other)
    return kl_rows[0], head_grad.reshape(ds, vocab_dev)


def solution(mesh):
    axes = ("y", "xh", "xl", "c", "z")
    fine = Mesh(mesh.devices.reshape(4, 2, 2, 2, 16), axes)
    tok = axes[:4]
    in_specs = (P(tok, "z"), P(tok, "z"), P(None, axes), P(None, axes), P(), P(), P(), P())
    out_specs = (P(tok), P(None, axes))
    return jax.shard_map(
        on_device, mesh=fine, in_specs=in_specs, out_specs=out_specs, check_vma=False
    )
```

time: 130 us -> 121 us (0.931); the launches traced: 128 us -> 121 us
  waiting for transfers between devices: 13.6 us -> 7.46 us
  blocking collectives: 86.3 us -> 84.1 us
    all_to_all x1, waiting for transfers between devices: 11.4 us -> 5.32 us  [on_device(): near = lax.all_to_all(quarters, tok, 0, 0)]
    all_to_all x1, blocking collectives: 30.4 us -> 28.1 us  [on_device(): lax.all_to_all(copies, ('xl', 'y', 'xh'), 0, 0).reshape(2, LIVE, quarter)]
    pallas_call x1 -> x3, Pallas kernels: 0.27 us -> 1.85 us  [the longest x1 0.91 us: on_device(): pl.pallas_call(index_kernel, out_shape=(jax.ShapeDtypeStruct((2, ROWS, ro...]
  transfers between devices with their start and end apart: 2 -> 2, of which waited for: 2 -> 2; matrix products, arithmetic and copies ran while one was open for 0% -> 1% of each run, Pallas kernels for 1% -> 2%
where the time goes in v4:
time: 121 us
  blocking collectives  84.1 us (70%)
  starting transfers between devices  17.2 us (14%)
  Pallas kernels  8.21 us (7%)
  waiting for transfers between devices  7.46 us (6%)
  local copies, waits for them, and re-layouts  2.46 us (2%)
    all_to_all x1, blocking collectives, on_device(): lax.all_to_all(copies, ('xl', 'y', 'xh'), 0, 0).reshape(2, LIVE, quarter)  28.1 us
    all_to_all x1, blocking collectives, on_device(): gathered = lax.all_to_all(picked, 'z', 0, 0)  25.1 us
    all_to_all x1, blocking collectives, on_device(): parts = lax.all_to_all(merged, 'z', 0, 0)  19.6 us
    all_to_all x1, blocking collectives, on_device(): parts = lax.all_to_all(stats, tok, 0, 0)  11.3 us
    all_to_all x1, starting transfers between devices, on_device(): near = lax.all_to_all(quarters, tok, 0, 0)  10.4 us
    ppermute x1, starting transfers between devices, on_device(): other = lax.ppermute(own, 'c', [(0, 1), (1, 0)])  6.8 us
    all_to_all x1, waiting for transfers between devices, on_device(): near = lax.all_to_all(quarters, tok, 0, 0)  5.32 us
    pallas_call x1, Pallas kernels, on_device(): pl.pallas_call(grad_kernel, out_shape=(jax.ShapeDtypeStruct((1, grp_rows)...  2.82 us
  transfers between devices with their start and end apart: 2, of which 2 were waited for; matrix products, arithmetic and copies ran while one was open for 1% of the time, Pallas kernels for 2%

profile of v4, /device:TPU:1, one launch (start us, length us, event | category | flops | bytes accessed | tf_op | source)
XLA Modules:
  0.0 120.9 jit_solution(10263024637380184807)
XLA Ops:
  0.6 0.0 copy-start
  0.6 0.7 copy-done
  1.3 0.0 copy-start.1
  1.3 0.7 copy-done.1
  2.0 0.8 shard_map.95
  2.8 10.4 %all-to-all-start = ((bf16[32,16,104]{2,1,0:T(8,128)(2,1)}), bf16[32,16,104]{2,1,0:T(8,128)(2,1)S(1)}, u32[]{:S(2)}, u32[]{:S(2)}) async-start(bf16[32,16,104]{2,1,0:T(8,128)(2,1)} %shard_map.95), calls=%async_computation | async-start | bytes 262144 | tf_op jit(solution)/shard_map/all_to_all | solution.py:200
  13.2 0.7 concatenate.3.table.where
  13.9 0.7 pad_add_fusion.rows
  14.7 0.9 shard_map.96
  15.6 5.3 %all-to-all-done.near = bf16[32,16,104]{2,1,0:T(8,128)(2,1)S(1)} async-done(((bf16[32,16,104]{2,1,0:T(8,128)(2,1)}), bf16[32,16,104]{2,1,0:T(8,128)(2,1)S(1)}, u32[]{:S(2)}, u32[]{:S(2)}) %all-to-all-start) | async-done | bytes 106528 | tf_op jit(solution)/shard_map/all_to_all | solution.py:200
  20.9 0.3 shard_map.97
  21.2 25.1 %all_to_all.25.gathered = bf16[16,40,104]{2,1,0:T(8,128)(2,1)S(1)} all-to-all(bf16[16,40,104]{2,1,0:T(8,128)(2,1)S(1)} %shard_map.97), channel_id=1, replica_groups=mesh['y'=4,'xh'=2,'xl'=2,'c'=2,'z'=16] {'z'}, dimensions={0} | all-to-all | bytes 266240 | tf_op jit(solution)/shard_map/all_to_all | solution.py:212
  46.3 0.2 shard_map.98
  46.6 0.0 copy-start.3
  46.6 28.1 %all_to_all.26 = bf16[16,40,1664]{2,1,0:T(8,128)(2,1)S(1)} all-to-all(bf16[16,40,1664]{2,1,0:T(8,128)(2,1)S(1)} %shard_map.98), channel_id=1, replica_groups=mesh['y'=4,'xh'=2,'xl'=2,'c'=2,'z'=16] {'xl','y','xh'}, dimensions={0} | all-to-all | bytes 4259840 | tf_op jit(solution)/shard_map/all_to_all | solution.py:218
  74.7 0.0 copy-start.2
  74.7 6.8 %collective-permute-start = (bf16[2,320,1664]{2,1,0:T(8,128)(2,1)S(1)}, bf16[2,320,1664]{2,1,0:T(8,128)(2,1)S(1)}, u32[]{:S(2)}, u32[]{:S(2)}) collective-permute-start(bf16[2,320,1664]{2,1,0:T(8,128)(2,1)S(1)} %bitcast.19), channel_id=1, source_target_pairs={{0,16},{16,0},{1,17},{17,1},{2,18},{18,2},{3,19},{19,3},{4,20},{20... | collective-permute-start | bytes 6389768 | tf_op jit(solution)/shard_map/ppermute | solution.py:219
  81.5 0.0 copy-done.3
  81.5 0.1 copy.10
  81.6 0.0 copy-done.2
  81.6 0.2 copy.11
  81.8 1.3 %shard_map.99 = (f32[320,256]{1,0:T(8,128)S(1)}, f32[320,256]{1,0:T(8,128)S(1)}) custom-call(s32[37]{0:T(128)S(1)} %concatenate.3.table.where, bf16[2,320,1664]{2,1,0:T(8,128)(2,1)S(1)} %bitcast.20, bf16[4,640,256]{2,1,0:T(8,128)(2,1)S(1)} %bitcast.24, bf16[4,1024,256]{2,1,0:T(8,128)(2,1)S(1)} %bitcast.22), custom_call_target="tpu_custom_call" | custom-call | tf_op jit(solution)/shard_map/pallas_call | solution.py:225
  83.1 2.1 %collective-permute-done.rows.other = bf16[2,320,1664]{2,1,0:T(8,128)(2,1)S(1)} collective-permute-done((bf16[2,320,1664]{2,1,0:T(8,128)(2,1)S(1)}, bf16[2,320,1664]{2,1,0:T(8,128)(2,1)S(1)}, u32[]{:S(2)}, u32[]{:S(2)}) %collective-permute-start) | collective-permute-done | bytes 2129952 | tf_op jit(solution)/shard_map/ppermute | solution.py:219
  85.3 1.7 %shard_map.100 = (f32[256,320]{1,0:T(8,128)S(1)}, f32[256,320]{1,0:T(8,128)S(1)}, f32[32,1,1280]{2,1,0:T(1,128)S(1)}) custom-call(s32[37]{0:T(128)S(1)} %concatenate.3.table.where, bf16[2,320,1664]{2,1,0:T(8,128)(2,1)S(1)} %collective-permute-done.rows.other, bf16[4,640,256]{2,1,0:T(8,128)(2,1)S(1)} %bitcast.25, bf16[4,1024,256]{2,1,0:T(8,128)(2,1)S(1)} %bitcast.23, ...), custom_call_target="tpu_custom_call" | custom-call | tf_op jit(solution)/shard_map/pallas_call | solution.py:230
  87.0 11.3 %all_to_all.27.parts = f32[32,1,1280]{2,1,0:T(1,128)S(1)} all-to-all(f32[32,1,1280]{2,1,0:T(1,128)S(1)} %get-tuple-element.16), channel_id=1, replica_groups=mesh['y'=4,'xh'=2,'xl'=2,'c'=2,'z'=16] {'y','xh','xl','c'}, dimensions={0} | all-to-all | bytes 327680 | tf_op jit(solution)/shard_map/all_to_all | solution.py:235
  98.3 0.2 shard_map.101
  98.5 19.6 %all_to_all.28.parts = f32[16,1,1280]{2,1,0:T(1,128)S(1)} all-to-all(f32[16,1,1280]{2,1,0:T(1,128)S(1)} %shard_map.101), channel_id=1, replica_groups=mesh['y'=4,'xh'=2,'xl'=2,'c'=2,'z'=16] {'z'}, dimensions={0} | all-to-all | bytes 163840 | tf_op jit(solution)/shard_map/all_to_all | solution.py:241
  118.1 2.8 %shard_map.102 = (f32[1,16]{1,0:T(1,128)}, bf16[16,4,40,256]{3,2,1,0:T(8,128)(2,1)}) custom-call(s32[37]{0:T(128)S(1)} %concatenate.3.table.where, f32[16,1,1280]{2,1,0:T(1,128)S(1)} %all_to_all.28.parts, f32[256,320]{1,0:T(8,128)S(1)} %get-tuple-element.17.s_t, f32[256,320]{1,0:T(8,128)S(1)} %get-tuple-element.18.u_t, s32[1,320]{1,0:T(1,128)S(1)} %get-tuple-element.19.mark, ...), custom_call_target="tpu_custom_call" | custom-call | tf_op jit(solution)/shard_map/pallas_call | solution.py:242
Async XLA Ops:
  0.6 0.7 copy-start
  1.3 0.7 copy-start.1
  2.8 18.1 %all-to-all-start = ((bf16[32,16,104]{2,1,0:T(8,128)(2,1)}), bf16[32,16,104]{2,1,0:T(8,128)(2,1)S(1)}, u32[]{:S(2)}, u32[]{:S(2)}) async-start(bf16[32,16,104]{2,1,0:T(8,128)(2,1)} %shard_map.95), calls=%async_computation | async-start | bytes 262144 | tf_op jit(solution)/shard_map/all_to_all | solution.py:200
  46.6 34.9 %copy-start.3 = (bf16[2560,256]{1,0:T(8,128)(2,1)S(1)}, bf16[2560,256]{1,0:T(8,128)(2,1)}, u32[]{:S(2)}) copy-start(bf16[2560,256]{1,0:T(8,128)(2,1)} %param.10) | copy-start | bytes 3932164
  74.7 6.9 %copy-start.2 = (bf16[4096,256]{1,0:T(8,128)(2,1)S(1)}, bf16[4096,256]{1,0:T(8,128)(2,1)}, u32[]{:S(2)}) copy-start(bf16[4096,256]{1,0:T(8,128)(2,1)} %param.11) | copy-start | bytes 6291460
  74.7 10.6 %collective-permute-start = (bf16[2,320,1664]{2,1,0:T(8,128)(2,1)S(1)}, bf16[2,320,1664]{2,1,0:T(8,128)(2,1)S(1)}, u32[]{:S(2)}, u32[]{:S(2)}) collective-permute-start(bf16[2,320,1664]{2,1,0:T(8,128)(2,1)S(1)} %bitcast.19), channel_id=1, source_target_pairs={{0,16},{16,0},{1,17},{17,1},{2,18},{18,2},{3,19},{19,3},{4,20},{20... | collective-permute-start | bytes 6389768 | tf_op jit(solution)/shard_map/ppermute | solution.py:219

commit v5 on v4

--- a/solution.py
+++ b/solution.py
@@ -34,15 +34,8 @@
     return rank
 
 
-def quarter_kernel(teacher_in, student_in, out, teacher, student, arrived):
-    loads = [
-        pltpu.make_async_copy(teacher_in, teacher, arrived.at[0]),
-        pltpu.make_async_copy(student_in, student, arrived.at[1]),
-    ]
-    for load in loads:
-        load.start()
-    for load in loads:
-        load.wait()
+def quarter_kernel(local, out):
+    teacher, student = local[:, : 4 * QT], local[:, 4 * QT :]
     blocks = []
     for q in range(4):
         part = [teacher[:, QT * q : QT * q + QT], student[:, QS * q : QS * q + QS]]
@@ -95,8 +88,10 @@
     return s, u
 
 
-def half_kernel(where, rows, head_s, head_t, s_out, u_out):
+def half_kernel(where, rows, head_s, head_t, s_out, u_out, turned):
     s_out[...], u_out[...] = logits_of(rows, head_s, head_t, where[0])
+    for i in range(2):
+        turned[i] = rows[i, :, head_t.shape[1] :].T
 
 
 def stats_kernel(
@@ -145,21 +140,30 @@
         out[i] = block
 
 
-def grad_kernel(table, parts, s_t, u_t, mark, own, other, kl_out, grad_out):
+def grad_kernel(
+    table, parts, s_t, u_t, mark, turned, other, kl_out, grad_out, ready, sent
+):
     core, group = table[0], table[2]
     nz = grad_out.shape[0]
-    dt = own.shape[2] - nz * QS
+    dt = other.shape[2] - nz * QS
     lse_s, lse_u, kl, apart = merge(parts[...])
     mixed = 1.0 / (0.2 * jnp.exp(apart - lse_u + lse_s) + 0.8)
     weight = jnp.where(mark[...] == 1, mixed, jnp.ones_like(mixed))
     log_s = s_t[...] - lse_s
     gap = log_s - (u_t[...] - lse_u)
     d_t = (weight * jnp.exp(log_s) * (gap - kl)).astype(BF16)
-    for half, rows in ((core, own), (1 - core, other)):
-        for i in range(2):
-            total = dot(d_t, rows[i, :, dt:]).T
-            for z in range(nz):
-                grad_out[z, 2 * half + i] = total[QS * z : QS * z + QS].astype(BF16)
+    leaving = []
+    for n in range(4):
+        if n < 2:
+            block = dot(turned[n], d_t, ((1,), (1,)))
+        else:
+            block = dot(d_t, other[n - 2, :, dt:]).T
+        for z in range(nz):
+            ready[n, z] = block[QS * z : QS * z + QS].astype(BF16)
+        half = core if n < 2 else 1 - core
+        copy = pltpu.make_async_copy(ready.at[n], grad_out.at[:, 2 * half + n % 2], sent.at[n])
+        copy.start()
+        leaving.append(copy)
     start = jnp.int32(0)
     for w in range(table.shape[0] - 5):
         start = start + jnp.where(w < group, table[5 + w], 0)
@@ -168,6 +172,8 @@
     mine = jnp.logical_and(column == row + start, row < table[5 + group])
     mine = jnp.sum(jnp.where(mine, kl, 0.0), axis=1, keepdims=True)
     kl_out[...] = jnp.broadcast_to(mine, (16, 128)).T[0:1]
+    for copy in leaving:
+        copy.wait()
 
 
 def on_device(
@@ -190,13 +196,8 @@
     quarters = pl.pallas_call(
         quarter_kernel,
         out_shape=jax.ShapeDtypeStruct((32, grp_rows, QT + QS), BF16),
-        in_specs=[pl.BlockSpec(memory_space=pltpu.HBM)] * 2, out_specs=VMEM,
-        scratch_shapes=[
-            pltpu.VMEM(teacher_rows.shape, BF16), pltpu.VMEM(student_hidden.shape, BF16),
-            pltpu.SemaphoreType.DMA((2,)),
-        ],
-        compiler_params=grant(4),
-    )(teacher_rows, student_hidden)
+        in_specs=[VMEM], out_specs=VMEM, compiler_params=grant(4),
+    )(jnp.concatenate([teacher_rows, student_hidden], axis=1))
     near = lax.all_to_all(quarters, tok, 0, 0)
     per_row = jax.ShapeDtypeStruct((1, LIVE), jnp.int32)
     pick, wanted, mark = pl.pallas_call(
@@ -222,9 +223,10 @@
     head_t = teacher_head.reshape(nz, 4, QT, vocab_dev).transpose(1, 0, 2, 3)
     head_t = head_t.reshape(4, dt // 4, vocab_dev)
     logits = jax.ShapeDtypeStruct((LIVE, vocab_dev), F32)
-    s_own, u_own = pl.pallas_call(
-        half_kernel, out_shape=(logits, logits),
-        in_specs=[SMEM] + [VMEM] * 3, out_specs=(VMEM, VMEM), compiler_params=grant(8),
+    turned = jax.ShapeDtypeStruct((2, ds // 4, LIVE), BF16)
+    s_own, u_own, turned = pl.pallas_call(
+        half_kernel, out_shape=(logits, logits, turned),
+        in_specs=[SMEM] + [VMEM] * 3, out_specs=(VMEM,) * 3, compiler_params=grant(8),
     )(table, own, head_s, head_t)
     whole = jax.ShapeDtypeStruct((vocab_dev, LIVE), F32)
     s_t, u_t, stats = pl.pallas_call(
@@ -245,8 +247,13 @@
             jax.ShapeDtypeStruct((1, grp_rows), F32),
             jax.ShapeDtypeStruct((nz, 4, QS, vocab_dev), BF16),
         ),
-        in_specs=[SMEM] + [VMEM] * 6, out_specs=(VMEM,) * 2, compiler_params=grant(8),
-    )(table, parts, s_t, u_t, mark, own, other)
+        in_specs=[SMEM] + [VMEM] * 6,
+        out_specs=(VMEM, pl.BlockSpec(memory_space=pl.ANY)),
+        scratch_shapes=[
+            pltpu.VMEM((4, nz, QS, vocab_dev), BF16), pltpu.SemaphoreType.DMA((4,))
+        ],
+        compiler_params=grant(8),
+    )(table, parts, s_t, u_t, mark, turned, other)
     return kl_rows[0], head_grad.reshape(ds, vocab_dev)
 
 

time: 121 us -> 121 us (level)
  local copies, waits for them, and re-layouts: 2.46 us -> 1.07 us
    unnamed x8 -> x4, local copies, waits for them, and re-layouts: 1.4 us -> 0.01 us
where the time goes in v5:
time: 121 us
  blocking collectives  84.3 us (70%)
  starting transfers between devices  17.1 us (14%)
  Pallas kernels  8.44 us (7%)
  waiting for transfers between devices  7.45 us (6%)
  other arithmetic  1.45 us (1%)
    all_to_all x1, blocking collectives, on_device(): lax.all_to_all(copies, ('xl', 'y', 'xh'), 0, 0).reshape(2, LIVE, quarter)  28.1 us
    all_to_all x1, blocking collectives, on_device(): gathered = lax.all_to_all(picked, 'z', 0, 0)  25.1 us
    all_to_all x1, blocking collectives, on_device(): parts = lax.all_to_all(merged, 'z', 0, 0)  19.7 us
    all_to_all x1, blocking collectives, on_device(): parts = lax.all_to_all(stats, tok, 0, 0)  11.3 us
    all_to_all x1, starting transfers between devices, on_device(): near = lax.all_to_all(quarters, tok, 0, 0)  10.4 us
    ppermute x1, starting transfers between devices, on_device(): other = lax.ppermute(own, 'c', [(0, 1), (1, 0)])  6.79 us
    all_to_all x1, waiting for transfers between devices, on_device(): near = lax.all_to_all(quarters, tok, 0, 0)  5.32 us
    pallas_call x1, Pallas kernels, on_device(): pl.pallas_call(grad_kernel, out_shape=(jax.ShapeDtypeStruct((1, grp_rows)...  3.08 us
  transfers between devices with their start and end apart: 2, of which 2 were waited for; matrix products, arithmetic and copies ran while one was open for 1% of the time, Pallas kernels for 2%

profile of v5, /device:TPU:1, one launch (start us, length us, event | category | flops | bytes accessed | tf_op | source)
XLA Modules:
  0.0 120.6 jit_solution(8461201742698864199)
XLA Ops:
  0.6 0.7 pad_maximum_fusion.local
  1.4 0.7 shard_map.95
  2.1 10.4 %all-to-all-start = ((bf16[32,16,104]{2,1,0:T(8,128)(2,1)}), bf16[32,16,104]{2,1,0:T(8,128)(2,1)S(1)}, u32[]{:S(2)}, u32[]{:S(2)}) async-start(bf16[32,16,104]{2,1,0:T(8,128)(2,1)} %shard_map.95), calls=%async_computation | async-start | bytes 262144 | tf_op jit(solution)/shard_map/all_to_all | solution.py:201
  12.5 0.7 concatenate.6.table.where
  13.2 0.7 pad_add_fusion.rows
  13.9 0.9 shard_map.96
  14.8 5.3 %all-to-all-done.near = bf16[32,16,104]{2,1,0:T(8,128)(2,1)S(1)} async-done(((bf16[32,16,104]{2,1,0:T(8,128)(2,1)}), bf16[32,16,104]{2,1,0:T(8,128)(2,1)S(1)}, u32[]{:S(2)}, u32[]{:S(2)}) %all-to-all-start) | async-done | bytes 106528 | tf_op jit(solution)/shard_map/all_to_all | solution.py:201
  20.2 0.3 shard_map.97
  20.5 25.1 %all_to_all.25.gathered = bf16[16,40,104]{2,1,0:T(8,128)(2,1)S(1)} all-to-all(bf16[16,40,104]{2,1,0:T(8,128)(2,1)S(1)} %shard_map.97), channel_id=1, replica_groups=mesh['y'=4,'xh'=2,'xl'=2,'c'=2,'z'=16] {'z'}, dimensions={0} | all-to-all | bytes 266240 | tf_op jit(solution)/shard_map/all_to_all | solution.py:213
  45.6 0.2 shard_map.98
  45.8 0.0 copy-start.1
  45.9 28.1 %all_to_all.26 = bf16[16,40,1664]{2,1,0:T(8,128)(2,1)S(1)} all-to-all(bf16[16,40,1664]{2,1,0:T(8,128)(2,1)S(1)} %shard_map.98), channel_id=1, replica_groups=mesh['y'=4,'xh'=2,'xl'=2,'c'=2,'z'=16] {'xl','y','xh'}, dimensions={0} | all-to-all | bytes 4259840 | tf_op jit(solution)/shard_map/all_to_all | solution.py:219
  74.0 0.0 copy-start
  74.0 6.8 %collective-permute-start = (bf16[2,320,1664]{2,1,0:T(8,128)(2,1)S(1)}, bf16[2,320,1664]{2,1,0:T(8,128)(2,1)S(1)}, u32[]{:S(2)}, u32[]{:S(2)}) collective-permute-start(bf16[2,320,1664]{2,1,0:T(8,128)(2,1)S(1)} %bitcast.23), channel_id=1, source_target_pairs={{0,16},{16,0},{1,17},{17,1},{2,18},{18,2},{3,19},{19,3},{4,20},{20... | collective-permute-start | bytes 6389768 | tf_op jit(solution)/shard_map/ppermute | solution.py:220
  80.8 0.0 copy-done.1
  80.8 0.1 copy.10
  80.9 0.0 copy-done
  80.9 0.2 copy.11
  81.1 1.3 %shard_map.99 = (f32[320,256]{1,0:T(8,128)S(1)}, f32[320,256]{1,0:T(8,128)S(1)}, bf16[2,640,320]{2,1,0:T(8,128)(2,1)S(1)}) custom-call(s32[37]{0:T(128)S(1)} %concatenate.6.table.where, bf16[2,320,1664]{2,1,0:T(8,128)(2,1)S(1)} %bitcast.24, bf16[4,640,256]{2,1,0:T(8,128)(2,1)S(1)} %bitcast.21, bf16[4,1024,256]{2,1,0:T(8,128)(2,1)S(1)} %bitcast.19), custom_call_target="tpu_custom_call" | custom-call | tf_op jit(solution)/shard_map/pallas_call | solution.py:227
  82.4 2.1 %collective-permute-done.rows.other = bf16[2,320,1664]{2,1,0:T(8,128)(2,1)S(1)} collective-permute-done((bf16[2,320,1664]{2,1,0:T(8,128)(2,1)S(1)}, bf16[2,320,1664]{2,1,0:T(8,128)(2,1)S(1)}, u32[]{:S(2)}, u32[]{:S(2)}) %collective-permute-start) | collective-permute-done | bytes 2129952 | tf_op jit(solution)/shard_map/ppermute | solution.py:220
  84.6 1.7 %shard_map.100 = (f32[256,320]{1,0:T(8,128)S(1)}, f32[256,320]{1,0:T(8,128)S(1)}, f32[32,1,1280]{2,1,0:T(1,128)S(1)}) custom-call(s32[37]{0:T(128)S(1)} %concatenate.6.table.where, bf16[2,320,1664]{2,1,0:T(8,128)(2,1)S(1)} %collective-permute-done.rows.other, bf16[4,640,256]{2,1,0:T(8,128)(2,1)S(1)} %bitcast.22, bf16[4,1024,256]{2,1,0:T(8,128)(2,1)S(1)} %bitcast.20, ...), custom_call_target="tpu_custom_call" | custom-call | tf_op jit(solution)/shard_map/pallas_call | solution.py:232
  86.3 11.3 %all_to_all.27.parts = f32[32,1,1280]{2,1,0:T(1,128)S(1)} all-to-all(f32[32,1,1280]{2,1,0:T(1,128)S(1)} %get-tuple-element.17), channel_id=1, replica_groups=mesh['y'=4,'xh'=2,'xl'=2,'c'=2,'z'=16] {'y','xh','xl','c'}, dimensions={0} | all-to-all | bytes 327680 | tf_op jit(solution)/shard_map/all_to_all | solution.py:237
  97.6 0.2 shard_map.101
  97.8 19.7 %all_to_all.28.parts = f32[16,1,1280]{2,1,0:T(1,128)S(1)} all-to-all(f32[16,1,1280]{2,1,0:T(1,128)S(1)} %shard_map.101), channel_id=1, replica_groups=mesh['y'=4,'xh'=2,'xl'=2,'c'=2,'z'=16] {'z'}, dimensions={0} | all-to-all | bytes 163840 | tf_op jit(solution)/shard_map/all_to_all | solution.py:243
  117.5 3.1 %shard_map.102 = (f32[1,16]{1,0:T(1,128)}, bf16[16,4,40,256]{3,2,1,0:T(8,128)(2,1)}) custom-call(s32[37]{0:T(128)S(1)} %concatenate.6.table.where, f32[16,1,1280]{2,1,0:T(1,128)S(1)} %all_to_all.28.parts, f32[256,320]{1,0:T(8,128)S(1)} %get-tuple-element.18.s_t, f32[256,320]{1,0:T(8,128)S(1)} %get-tuple-element.19.u_t, s32[1,320]{1,0:T(1,128)S(1)} %get-tuple-element.20.mark, ...), custom_call_target="tpu_custom_call" | custom-call | tf_op jit(solution)/shard_map/pallas_call | solution.py:244
Async XLA Ops:
  2.1 18.1 %all-to-all-start = ((bf16[32,16,104]{2,1,0:T(8,128)(2,1)}), bf16[32,16,104]{2,1,0:T(8,128)(2,1)S(1)}, u32[]{:S(2)}, u32[]{:S(2)}) async-start(bf16[32,16,104]{2,1,0:T(8,128)(2,1)} %shard_map.95), calls=%async_computation | async-start | bytes 262144 | tf_op jit(solution)/shard_map/all_to_all | solution.py:201
  45.8 34.9 %copy-start.1 = (bf16[2560,256]{1,0:T(8,128)(2,1)S(1)}, bf16[2560,256]{1,0:T(8,128)(2,1)}, u32[]{:S(2)}) copy-start(bf16[2560,256]{1,0:T(8,128)(2,1)} %param.10) | copy-start | bytes 3932164
  74.0 6.9 %copy-start = (bf16[4096,256]{1,0:T(8,128)(2,1)S(1)}, bf16[4096,256]{1,0:T(8,128)(2,1)}, u32[]{:S(2)}) copy-start(bf16[4096,256]{1,0:T(8,128)(2,1)} %param.11) | copy-start | bytes 6291460
  74.0 10.6 %collective-permute-start = (bf16[2,320,1664]{2,1,0:T(8,128)(2,1)S(1)}, bf16[2,320,1664]{2,1,0:T(8,128)(2,1)S(1)}, u32[]{:S(2)}, u32[]{:S(2)}) collective-permute-start(bf16[2,320,1664]{2,1,0:T(8,128)(2,1)S(1)} %bitcast.23), channel_id=1, source_target_pairs={{0,16},{16,0},{1,17},{17,1},{2,18},{18,2},{3,19},{19,3},{4,20},{20... | collective-permute-start | bytes 6389768 | tf_op jit(solution)/shard_map/ppermute | solution.py:220

commit v6 on v5

--- a/solution.py
+++ b/solution.py
@@ -141,7 +141,7 @@
 
 
 def grad_kernel(
-    table, parts, s_t, u_t, mark, turned, other, kl_out, grad_out, ready, sent
+    table, parts, s_t, u_t, mark, turned, other, kl_out, grad_out
 ):
     core, group = table[0], table[2]
     nz = grad_out.shape[0]
@@ -151,19 +151,15 @@
     weight = jnp.where(mark[...] == 1, mixed, jnp.ones_like(mixed))
     log_s = s_t[...] - lse_s
     gap = log_s - (u_t[...] - lse_u)
-    d_t = (weight * jnp.exp(log_s) * (gap - kl)).astype(BF16)
-    leaving = []
+    d = (weight * jnp.exp(log_s) * (gap - kl)).T.astype(BF16)
     for n in range(4):
         if n < 2:
-            block = dot(turned[n], d_t, ((1,), (1,)))
+            block = dot(turned[n], d)
         else:
-            block = dot(d_t, other[n - 2, :, dt:]).T
+            block = dot(other[n - 2, :, dt:], d, ((0,), (0,)))
+        half = core if n < 2 else 1 - core
         for z in range(nz):
-            ready[n, z] = block[QS * z : QS * z + QS].astype(BF16)
-        half = core if n < 2 else 1 - core
-        copy = pltpu.make_async_copy(ready.at[n], grad_out.at[:, 2 * half + n % 2], sent.at[n])
-        copy.start()
-        leaving.append(copy)
+            grad_out[z, 2 * half + n % 2] = block[QS * z : QS * z + QS].astype(BF16)
     start = jnp.int32(0)
     for w in range(table.shape[0] - 5):
         start = start + jnp.where(w < group, table[5 + w], 0)
@@ -172,8 +168,6 @@
     mine = jnp.logical_and(column == row + start, row < table[5 + group])
     mine = jnp.sum(jnp.where(mine, kl, 0.0), axis=1, keepdims=True)
     kl_out[...] = jnp.broadcast_to(mine, (16, 128)).T[0:1]
-    for copy in leaving:
-        copy.wait()
 
 
 def on_device(
@@ -248,10 +242,7 @@
             jax.ShapeDtypeStruct((nz, 4, QS, vocab_dev), BF16),
         ),
         in_specs=[SMEM] + [VMEM] * 6,
-        out_specs=(VMEM, pl.BlockSpec(memory_space=pl.ANY)),
-        scratch_shapes=[
-            pltpu.VMEM((4, nz, QS, vocab_dev), BF16), pltpu.SemaphoreType.DMA((4,))
-        ],
+        out_specs=(VMEM,) * 2,
         compiler_params=grant(8),
     )(table, parts, s_t, u_t, mark, turned, other)
     return kl_rows[0], head_grad.reshape(ds, vocab_dev)

time: 121 us -> 121 us (level)
  no operation moved by 1% of the time
where the time goes in v6:
time: 121 us; the launch traced here: 120 us
  blocking collectives  84.3 us (70%)
  starting transfers between devices  17.1 us (14%)
  Pallas kernels  8.12 us (7%)
  waiting for transfers between devices  7.45 us (6%)
  other arithmetic  1.45 us (1%)
    all_to_all x1, blocking collectives, on_device(): lax.all_to_all(copies, ('xl', 'y', 'xh'), 0, 0).reshape(2, LIVE, quarter)  28.1 us
    all_to_all x1, blocking collectives, on_device(): gathered = lax.all_to_all(picked, 'z', 0, 0)  25.1 us
    all_to_all x1, blocking collectives, on_device(): parts = lax.all_to_all(merged, 'z', 0, 0)  19.7 us
    all_to_all x1, blocking collectives, on_device(): parts = lax.all_to_all(stats, tok, 0, 0)  11.3 us
    all_to_all x1, starting transfers between devices, on_device(): near = lax.all_to_all(quarters, tok, 0, 0)  10.4 us
    ppermute x1, starting transfers between devices, on_device(): other = lax.ppermute(own, 'c', [(0, 1), (1, 0)])  6.79 us
    all_to_all x1, waiting for transfers between devices, on_device(): near = lax.all_to_all(quarters, tok, 0, 0)  5.32 us
    pallas_call x1, Pallas kernels, on_device(): pl.pallas_call(grad_kernel, out_shape=(jax.ShapeDtypeStruct((1, grp_rows)...  2.75 us
  transfers between devices with their start and end apart: 2, of which 2 were waited for; matrix products, arithmetic and copies ran while one was open for 1% of the time, Pallas kernels for 2%

profile of v6, /device:TPU:1, one launch (start us, length us, event | category | flops | bytes accessed | tf_op | source)
XLA Modules:
  0.0 120.2 jit_solution(10287395744285128676)
XLA Ops:
  0.6 0.7 pad_maximum_fusion.local
  1.4 0.7 shard_map.95
  2.1 10.4 %all-to-all-start = ((bf16[32,16,104]{2,1,0:T(8,128)(2,1)}), bf16[32,16,104]{2,1,0:T(8,128)(2,1)S(1)}, u32[]{:S(2)}, u32[]{:S(2)}) async-start(bf16[32,16,104]{2,1,0:T(8,128)(2,1)} %shard_map.95), calls=%async_computation | async-start | bytes 262144 | tf_op jit(solution)/shard_map/all_to_all | solution.py:195
  12.5 0.7 concatenate.6.table.where
  13.2 0.7 pad_add_fusion.rows
  13.9 0.9 shard_map.96
  14.8 5.3 %all-to-all-done.near = bf16[32,16,104]{2,1,0:T(8,128)(2,1)S(1)} async-done(((bf16[32,16,104]{2,1,0:T(8,128)(2,1)}), bf16[32,16,104]{2,1,0:T(8,128)(2,1)S(1)}, u32[]{:S(2)}, u32[]{:S(2)}) %all-to-all-start) | async-done | bytes 106528 | tf_op jit(solution)/shard_map/all_to_all | solution.py:195
  20.2 0.3 shard_map.97
  20.5 25.1 %all_to_all.25.gathered = bf16[16,40,104]{2,1,0:T(8,128)(2,1)S(1)} all-to-all(bf16[16,40,104]{2,1,0:T(8,128)(2,1)S(1)} %shard_map.97), channel_id=1, replica_groups=mesh['y'=4,'xh'=2,'xl'=2,'c'=2,'z'=16] {'z'}, dimensions={0} | all-to-all | bytes 266240 | tf_op jit(solution)/shard_map/all_to_all | solution.py:207
  45.6 0.2 shard_map.98
  45.8 0.0 copy-start.1
  45.9 28.1 %all_to_all.26 = bf16[16,40,1664]{2,1,0:T(8,128)(2,1)S(1)} all-to-all(bf16[16,40,1664]{2,1,0:T(8,128)(2,1)S(1)} %shard_map.98), channel_id=1, replica_groups=mesh['y'=4,'xh'=2,'xl'=2,'c'=2,'z'=16] {'xl','y','xh'}, dimensions={0} | all-to-all | bytes 4259840 | tf_op jit(solution)/shard_map/all_to_all | solution.py:213
  74.0 0.0 copy-start
  74.0 6.8 %collective-permute-start = (bf16[2,320,1664]{2,1,0:T(8,128)(2,1)S(1)}, bf16[2,320,1664]{2,1,0:T(8,128)(2,1)S(1)}, u32[]{:S(2)}, u32[]{:S(2)}) collective-permute-start(bf16[2,320,1664]{2,1,0:T(8,128)(2,1)S(1)} %bitcast.23), channel_id=1, source_target_pairs={{0,16},{16,0},{1,17},{17,1},{2,18},{18,2},{3,19},{19,3},{4,20},{20... | collective-permute-start | bytes 6389768 | tf_op jit(solution)/shard_map/ppermute | solution.py:214
  80.8 0.0 copy-done.1
  80.8 0.1 copy.10
  80.9 0.0 copy-done
  80.9 0.2 copy.11
  81.1 1.3 %shard_map.99 = (f32[320,256]{1,0:T(8,128)S(1)}, f32[320,256]{1,0:T(8,128)S(1)}, bf16[2,640,320]{2,1,0:T(8,128)(2,1)S(1)}) custom-call(s32[37]{0:T(128)S(1)} %concatenate.6.table.where, bf16[2,320,1664]{2,1,0:T(8,128)(2,1)S(1)} %bitcast.24, bf16[4,640,256]{2,1,0:T(8,128)(2,1)S(1)} %bitcast.21, bf16[4,1024,256]{2,1,0:T(8,128)(2,1)S(1)} %bitcast.19), custom_call_target="tpu_custom_call" | custom-call | tf_op jit(solution)/shard_map/pallas_call | solution.py:221
  82.4 2.1 %collective-permute-done.rows.other = bf16[2,320,1664]{2,1,0:T(8,128)(2,1)S(1)} collective-permute-done((bf16[2,320,1664]{2,1,0:T(8,128)(2,1)S(1)}, bf16[2,320,1664]{2,1,0:T(8,128)(2,1)S(1)}, u32[]{:S(2)}, u32[]{:S(2)}) %collective-permute-start) | collective-permute-done | bytes 2129952 | tf_op jit(solution)/shard_map/ppermute | solution.py:214
  84.6 1.7 %shard_map.100 = (f32[256,320]{1,0:T(8,128)S(1)}, f32[256,320]{1,0:T(8,128)S(1)}, f32[32,1,1280]{2,1,0:T(1,128)S(1)}) custom-call(s32[37]{0:T(128)S(1)} %concatenate.6.table.where, bf16[2,320,1664]{2,1,0:T(8,128)(2,1)S(1)} %collective-permute-done.rows.other, bf16[4,640,256]{2,1,0:T(8,128)(2,1)S(1)} %bitcast.22, bf16[4,1024,256]{2,1,0:T(8,128)(2,1)S(1)} %bitcast.20, ...), custom_call_target="tpu_custom_call" | custom-call | tf_op jit(solution)/shard_map/pallas_call | solution.py:226
  86.3 11.3 %all_to_all.27.parts = f32[32,1,1280]{2,1,0:T(1,128)S(1)} all-to-all(f32[32,1,1280]{2,1,0:T(1,128)S(1)} %get-tuple-element.17), channel_id=1, replica_groups=mesh['y'=4,'xh'=2,'xl'=2,'c'=2,'z'=16] {'y','xh','xl','c'}, dimensions={0} | all-to-all | bytes 327680 | tf_op jit(solution)/shard_map/all_to_all | solution.py:231
  97.6 0.2 shard_map.101
  97.8 19.7 %all_to_all.28.parts = f32[16,1,1280]{2,1,0:T(1,128)S(1)} all-to-all(f32[16,1,1280]{2,1,0:T(1,128)S(1)} %shard_map.101), channel_id=1, replica_groups=mesh['y'=4,'xh'=2,'xl'=2,'c'=2,'z'=16] {'z'}, dimensions={0} | all-to-all | bytes 163840 | tf_op jit(solution)/shard_map/all_to_all | solution.py:237
  117.5 2.8 %shard_map.102 = (f32[1,16]{1,0:T(1,128)}, bf16[16,4,40,256]{3,2,1,0:T(8,128)(2,1)}) custom-call(s32[37]{0:T(128)S(1)} %concatenate.6.table.where, f32[16,1,1280]{2,1,0:T(1,128)S(1)} %all_to_all.28.parts, f32[256,320]{1,0:T(8,128)S(1)} %get-tuple-element.18.s_t, f32[256,320]{1,0:T(8,128)S(1)} %get-tuple-element.19.u_t, s32[1,320]{1,0:T(1,128)S(1)} %get-tuple-element.20.mark, ...), custom_call_target="tpu_custom_call" | custom-call | tf_op jit(solution)/shard_map/pallas_call | solution.py:238
Async XLA Ops:
  2.1 18.1 %all-to-all-start = ((bf16[32,16,104]{2,1,0:T(8,128)(2,1)}), bf16[32,16,104]{2,1,0:T(8,128)(2,1)S(1)}, u32[]{:S(2)}, u32[]{:S(2)}) async-start(bf16[32,16,104]{2,1,0:T(8,128)(2,1)} %shard_map.95), calls=%async_computation | async-start | bytes 262144 | tf_op jit(solution)/shard_map/all_to_all | solution.py:195
  45.8 34.9 %copy-start.1 = (bf16[2560,256]{1,0:T(8,128)(2,1)S(1)}, bf16[2560,256]{1,0:T(8,128)(2,1)}, u32[]{:S(2)}) copy-start(bf16[2560,256]{1,0:T(8,128)(2,1)} %param.10) | copy-start | bytes 3932164
  74.0 6.9 %copy-start = (bf16[4096,256]{1,0:T(8,128)(2,1)S(1)}, bf16[4096,256]{1,0:T(8,128)(2,1)}, u32[]{:S(2)}) copy-start(bf16[4096,256]{1,0:T(8,128)(2,1)} %param.11) | copy-start | bytes 6291460
  74.0 10.6 %collective-permute-start = (bf16[2,320,1664]{2,1,0:T(8,128)(2,1)S(1)}, bf16[2,320,1664]{2,1,0:T(8,128)(2,1)S(1)}, u32[]{:S(2)}, u32[]{:S(2)}) collective-permute-start(bf16[2,320,1664]{2,1,0:T(8,128)(2,1)S(1)} %bitcast.23), channel_id=1, source_target_pairs={{0,16},{16,0},{1,17},{17,1},{2,18},{18,2},{3,19},{19,3},{4,20},{20... | collective-permute-start | bytes 6389768 | tf_op jit(solution)/shard_map/ppermute | solution.py:214
